TPU v7x, 128 devices: a whole 4x4x4 slice. The times are simulated.
128 devices in a mesh: lat: 8 (over x, core), lon: 16 (over z, y).
Axes of the slice: x: 4, y: 4, z: 4, core: 2. Of those that a mesh axis runs over, the one named last changes fastest.
Arguments:
- adjoint_in: bfloat16 [256, 64, 4096], P(None, 'lat', 'lon'), may hold values from -6 to 6
- layer_input: bfloat16 [256, 64, 4096], P(None, 'lat', 'lon'), may hold values from -6 to 6
- conv_weight: bfloat16 [8, 9, 32, 32], replicated, may hold values from -0.375 to 0.375
- footprint: int32 [2048, 64], P(('lat', 'lon')), may hold values from 0 to 262143, as said below
- owner: int32 [2048, 1], P(('lat', 'lon')), may hold values from 0 to 15; in each aligned block of 16 rows (0 to 15, 16 to 31, ...) at most 2 rows name the same one
- obs_weight: bfloat16 [4096, 32, 64], P(('lat', 'lon')), may hold values from -0.75 to 0.75
- obs_value: bfloat16 [4096, 32, 256], P(('lat', 'lon')), may hold values from -6 to 6
- obs_precision: bfloat16 [4096, 256], P(('lat', 'lon')), may hold values from 0.25 to 4
- obs_count: int32 [4096], P(('lat', 'lon')), may hold values from 1 to 32
Outputs:
- adjoint_out: bfloat16 [256, 64, 4096], P(None, 'lat', 'lon')
- weight_grad: float32 [8, 9, 32, 32], replicated
Inputs may be any that keep to these rules, and one draw needn't show every extreme that they name: `footprint`: the cells of one track form a 8 x 8 square of the grid lying inside the block of cells of the device that holds the track. Among the 16 tracks of one device no owner is named more than 2 times.
All inputs are finite; a program needn't handle non-finite values.
Results may differ from a plain program's by a relative error of at most 0.0045.
Values may be sent and summed in bfloat16 or wider, within the bound.
A program may use at most 128 MiB of HBM per device.

v0:
```python
import math

import jax
import jax.numpy as jnp
from jax import lax
from jax.sharding import PartitionSpec as P


def with_halo(block, sides, width, periodic):
    for axis, dim in sides:
        count = lax.axis_size(axis)
        forward = [(i, i + 1) for i in range(count - 1)]
        if periodic:
            forward.append((count - 1, 0))
        backward = [(target, source) for source, target in forward]
        low = lax.ppermute(
            lax.slice_in_dim(block, block.shape[dim] - width, None, axis=dim), axis, forward
        )
        high = lax.ppermute(lax.slice_in_dim(block, 0, width, axis=dim), axis, backward)
        block = jnp.concatenate([low, block, high], axis=dim)
    return block


def widen(source_field):
    lat_wide = with_halo(source_field, (("lat", 2),), 2, False)
    return with_halo(lat_wide, (("lon", 3),), 2, True)


def on_device(
    adjoint_in,
    layer_input,
    conv_weight,
    footprint,
    owner,
    obs_weight,
    obs_value,
    obs_precision,
    obs_count,
):
    channels, height, width = adjoint_in.shape
    groups, tap_count, group_size, _ = conv_weight.shape
    lat_count = lax.axis_size("lat")
    lon_count = lax.axis_size("lon")
    cells = height * width
    adjoint_local = adjoint_in.reshape(groups, group_size, cells)
    extended = widen(jnp.stack([adjoint_in, layer_input]))
    adjoint_wide = extended[0]
    input_wide = extended[1]
    backward = jnp.zeros((groups, group_size, cells), jnp.float32)
    tap_grads = []
    for row_tap in range(3):
        for col_tap in range(3):
            tap_index = 3 * row_tap + col_tap
            shifted = adjoint_wide[
                :,
                4 - 2 * row_tap : 4 - 2 * row_tap + height,
                4 - 2 * col_tap : 4 - 2 * col_tap + width,
            ]
            shifted = shifted.reshape(groups, group_size, cells)
            backward = backward + jnp.einsum(
                "gio,gon->gin",
                conv_weight[:, tap_index],
                shifted,
                preferred_element_type=jnp.float32,
            )
            moved_input = input_wide[
                :, 2 * row_tap : 2 * row_tap + height, 2 * col_tap : 2 * col_tap + width
            ]
            moved_input = moved_input.reshape(groups, group_size, cells)
            tap_grads.append(
                jnp.einsum(
                    "gin,gon->gio", moved_input, adjoint_local, preferred_element_type=jnp.float32
                )
            )
    local_grad = jnp.stack(tap_grads, axis=1)
    norm_factor = 1.0 / math.sqrt(cells * lat_count * lon_count)
    weight_grad = lax.psum(local_grad, ("lat", "lon")) * norm_factor
    tracks, points = footprint.shape
    slots = obs_weight.shape[0]
    obs_rows = obs_weight.shape[1]
    capacity = slots // lon_count
    lat_start = lax.axis_index("lat") * height
    lon_start = lax.axis_index("lon") * width
    full_width = width * lon_count
    local_cell = (footprint // full_width - lat_start) * width + (
        footprint % full_width - lon_start
    )
    pick_table = (
        local_cell.reshape(-1)[:, None] == jnp.arange(cells, dtype=jnp.int32)[None, :]
    ).astype(jnp.bfloat16)
    model_cells = lax.dot_general(
        layer_input.reshape(channels, cells),
        pick_table,
        (((1,), (1,)), ((), ())),
        preferred_element_type=jnp.float32,
    )
    values = model_cells.astype(jnp.bfloat16).T.reshape(tracks, points, channels)
    target = owner[:, 0]
    onehot = (target[:, None] == jnp.arange(lon_count, dtype=jnp.int32)[None, :]).astype(jnp.int32)
    position = jnp.sum((jnp.cumsum(onehot, axis=0) - onehot) * onehot, axis=1)
    slot_index = target * capacity + position
    select = (slot_index[None, :] == jnp.arange(slots, dtype=jnp.int32)[:, None]).astype(
        jnp.bfloat16
    )
    live_rows = jnp.arange(obs_rows, dtype=jnp.int32)[None, :] < obs_count[:, None]
    wmask = jnp.where(live_rows[:, :, None], obs_weight, jnp.zeros_like(obs_weight))
    outgoing = jnp.dot(
        select, values.reshape(tracks, points * channels), preferred_element_type=jnp.float32
    )
    outgoing = outgoing.astype(jnp.bfloat16).reshape(lon_count, capacity, points, channels)
    arrived = lax.all_to_all(outgoing, "lon", split_axis=0, concat_axis=0, tiled=True).reshape(
        slots, points, channels
    )
    model_obs = jnp.einsum("skp,spc->skc", wmask, arrived, preferred_element_type=jnp.float32)
    misfit = (
        (model_obs - obs_value.astype(jnp.float32)) * obs_precision.astype(jnp.float32)[:, None, :]
    ).astype(jnp.bfloat16)
    pulled = jnp.einsum("skp,skc->spc", wmask, misfit, preferred_element_type=jnp.float32).astype(
        jnp.bfloat16
    )
    pulled = pulled.reshape(lon_count, capacity, points, channels)
    returned = lax.all_to_all(pulled, "lon", split_axis=0, concat_axis=0, tiled=True).reshape(
        slots, points * channels
    )
    own_pull = jnp.dot(select.T, returned, preferred_element_type=jnp.float32).astype(jnp.bfloat16)
    obs_field = lax.dot_general(
        own_pull.reshape(tracks * points, channels),
        pick_table,
        (((0,), (0,)), ((), ())),
        preferred_element_type=jnp.float32,
    )
    total = (
        adjoint_in.astype(jnp.float32)
        + backward.reshape(channels, height, width)
        + obs_field.reshape(channels, height, width)
    )
    return (total.astype(jnp.bfloat16), weight_grad)


def solution(mesh):
    in_specs = (
        P(None, "lat", "lon"),
        P(None, "lat", "lon"),
        P(),
        P(("lat", "lon"), None),
        P(("lat", "lon"), None),
        P(("lat", "lon"), None, None),
        P(("lat", "lon"), None, None),
        P(("lat", "lon"), None),
        P(("lat", "lon")),
    )
    out_specs = (P(None, "lat", "lon"), P())
    return jax.shard_map(
        on_device, mesh=mesh, in_specs=in_specs, out_specs=out_specs, check_vma=False
    )
```

profile of v0, /device:TPU:1, one launch (start us, length us, event | category | flops | bytes accessed | tf_op | source)
XLA Modules:
  0.0 279.7 jit_solution(16948455938400442767)
XLA Ops:
  10.8 4.5 %collective-permute-start = (bf16[2,256,2,256]{1,3,2,0:T(8,128)(2,1)}, bf16[2,256,2,256]{1,3,2,0:T(8,128)(2,1)}, u32[]{:S(2)}, u32[]{:S(2)}) collective-permute-start(bf16[2,256,2,256]{1,3,2,0:T(8,128)(2,1)} %get-tuple-element.10), channel_id=1, source_target_pairs={{0,16},{16,32},{32,48},{48,64},{64,80},{80,96},{96,112},{1,17},{17... | collective-permute-start | bytes 1572872 | tf_op jit(solution)/shard_map/ppermute | solution.py:16
  18.9 2.8 fusion.12
  23.6 7.8 %all-to-all-start = ((bf16[16,2,64,256]{3,2,1,0:T(8,128)(2,1)}), bf16[16,2,64,256]{3,2,1,0:T(8,128)(2,1)}, u32[]{:S(2)}, u32[]{:S(2)}) async-start(bf16[16,2,64,256]{3,2,1,0:T(8,128)(2,1)} %bitcast.52), calls=%async_computation | async-start | bytes 2097152 | tf_op jit(solution)/shard_map/all_to_all | solution.py:111
  33.8 3.6 %collective-permute-start.3 = (bf16[2,256,12,2]{1,3,2,0:T(2,128)(2,1)S(1)}, bf16[2,256,12,2]{1,3,2,0:T(2,128)(2,1)S(1)}, u32[]{:S(2)}, u32[]{:S(2)}) collective-permute-start(bf16[2,256,12,2]{1,3,2,0:T(2,128)(2,1)S(1)} %get-tuple-element.9), channel_id=1, source_target_pairs={{1,0},{2,1},{3,2},{4,3},{5,4},{6,5},{7,6},{8,7},{9,8},{10,9},{11,1... | collective-permute-start | bytes 73736 | tf_op jit(solution)/shard_map/ppermute | solution.py:19
  38.9 8.6 %collective-permute-done.2 = bf16[2,256,12,2]{1,3,2,0:T(2,128)(2,1)S(1)} collective-permute-done((bf16[2,256,12,2]{1,3,2,0:T(2,128)(2,1)S(1)}, bf16[2,256,12,2]{1,3,2,0:T(2,128)(2,1)S(1)}, u32[]{:S(2)}, u32[]{:S(2)}) %collective-permute-start.2) | collective-permute-done | bytes 24608 | tf_op jit(solution)/shard_map/ppermute | solution.py:16
  47.5 2.7 pad_maximum_fusion
  50.5 7.2 %fusion.63 = (bf16[256,8,256]{0,2,1:T(8,128)(2,1)}, bf16[256,8,256]{0,2,1:T(8,128)(2,1)}, bf16[256,8,256]{0,2,1:T(8,128)(2,1)}, bf16[256,8,256]{0,2,1:T(8,128)(2...) fusion(bf16[256,12,260]{0,2,1:T(8,128)(2,1)S(1)} %get-tuple-ele, ...), kind=kLoop, calls=%fused_computation.102 | loop fusion | bytes 37748736 | tf_op jit(solution)/shard_map/slice | solution.py:66
  57.7 2.6 copy.48
  60.4 2.4 reshape.148
  62.7 2.6 copy.49
  65.4 2.4 reshape.150
  67.7 2.6 copy.50
  72.7 2.6 copy.51
  77.7 2.6 copy.52
  82.6 2.6 copy.53
  87.6 2.6 copy.54
  90.2 2.4 reshape.155
  92.6 2.6 copy.55
  95.2 2.3 reshape.156
  97.6 2.6 copy.56
  102.5 2.4 fusion.21
  116.8 2.7 copy.30
  119.5 2.4 reshape.133
  126.0 2.7 copy.34
  128.8 2.3 reshape.135
  132.9 2.4 reshape.136
  135.3 2.7 copy.38
  138.0 2.3 reshape.137
  157.8 3.4 %convolution_convert_fusion.2 = bf16[32,64,256]{2,1,0:T(8,128)(2,1)} fusion(bf16[32,64,256]{2,1,0:T(8,128)(2,1)} %bitcast.14, bf16[32,32,256]{2,1,0:T(8,128)(2,1)S(1)} %copy-done.23, f32[32,256]{1,0:T(8,128)S(1)} %convert_element_type.38, bf16[32,32,64]{2,1,0:T(8,128)(2,1)S(1)} %copy-done.21, pred[32,32]{1,0:T(8,128)(4,1)S(1)} %iota_compare_fusion.4), kind=kOutput, calls=%fused_computation.23 | convolution fusion | flops 68812800 | bytes 2786304 | tf_op jit(solution)/shard_map/skp,skc->spc/dot_general | solution.py:118
  161.2 6.8 %all-to-all-start.1 = ((bf16[16,2,64,256]{3,2,1,0:T(8,128)(2,1)}), bf16[16,2,64,256]{3,2,1,0:T(8,128)(2,1)S(1)}, u32[]{:S(2)}, u32[]{:S(2)}) async-start(bf16[16,2,64,256]{3,2,1,0:T(8,128)(2,1)} %bitcast.15), calls=%async_computation.1 | async-start | bytes 2097152 | tf_op jit(solution)/shard_map/all_to_all | solution.py:122
  173.3 90.8 %all-reduce.2.cloned.1.call-done = f32[8,9,32,32]{3,2,0,1:T(8,128)} async-done(((f32[8,9,32,32]{3,2,0,1:T(8,128)}), f32[8,9,32,32]{3,2,0,1:T(8,128)}) %all-reduce.2.cloned.1.call-update) | async-done | bytes 294928 | tf_op jit(solution)/shard_map/psum | solution.py:77
  267.8 3.5 %fusion.7 = bf16[256,8,256]{2,0,1:T(8,128)(2,1)S(1)} fusion(f32[256,8,256]{2,1,0:T(8,128)} %bitcast.148, s32[8,256]{1,0:T(8,128)S(1)} %multiply_add_fusion, s32[1024]{0:T(1024)S(1)} %eq.71, bf16[256,8,256]{2,1,0:T(8,128)(2,1)S(1)} %copy-done.5, bf16[1024,256]{1,0:T(8,128)(2,1)S(1)} %reshape.147), kind=kOutput, calls=%fused_computation.20 | convolution fusion | flops 1077936128 | bytes 4730880 | tf_op jit(solution)/shard_map/dot_general | solution.py:126
  (124 shorter events, 70.4 us)
Async XLA Ops:
  7.2 1.7 copy-start.4
  9.7 7.5 %copy-start.25 = (s32[16,64]{1,0:T(8,128)S(1)}, s32[16,64]{1,0:T(8,128)}, u32[]{:S(2)}) copy-start(s32[16,64]{1,0:T(8,128)} %param.12) | copy-start | bytes 12292
  9.7 8.9 %copy-start.26 = (s32[16,1]{0,1:T(1,128)S(1)}, s32[16,1]{0,1:T(1,128)}, u32[]{:S(2)}) copy-start(s32[16,1]{0,1:T(1,128)} %param.13) | copy-start | bytes 196
  10.8 20.8 %collective-permute-start = (bf16[2,256,2,256]{1,3,2,0:T(8,128)(2,1)}, bf16[2,256,2,256]{1,3,2,0:T(8,128)(2,1)}, u32[]{:S(2)}, u32[]{:S(2)}) collective-permute-start(bf16[2,256,2,256]{1,3,2,0:T(8,128)(2,1)} %get-tuple-element.10), channel_id=1, source_target_pairs={{0,16},{16,32},{32,48},{48,64},{64,80},{80,96},{96,112},{1,17},{17... | collective-permute-start | bytes 1572872 | tf_op jit(solution)/shard_map/ppermute | solution.py:16
  15.3 16.3 %collective-permute-start.1 = (bf16[2,256,2,256]{1,3,2,0:T(8,128)(2,1)}, bf16[2,256,2,256]{1,3,2,0:T(8,128)(2,1)}, u32[]{:S(2)}, u32[]{:S(2)}) collective-permute-start(bf16[2,256,2,256]{1,3,2,0:T(8,128)(2,1)} %get-tuple-element.11), channel_id=1, source_target_pairs={{16,0},{32,16},{48,32},{64,48},{80,64},{96,80},{112,96},{17,1},{33... | collective-permute-start | bytes 1572872 | tf_op jit(solution)/shard_map/ppermute | solution.py:19
  22.4 9.1 %copy-start.27 = (s32[32]{0:T(128)S(1)}, s32[32]{0:T(128)}, u32[]{:S(2)}) copy-start(s32[32]{0:T(128)} %param.17) | copy-start | bytes 388
  23.6 134.2 %all-to-all-start = ((bf16[16,2,64,256]{3,2,1,0:T(8,128)(2,1)}), bf16[16,2,64,256]{3,2,1,0:T(8,128)(2,1)}, u32[]{:S(2)}, u32[]{:S(2)}) async-start(bf16[16,2,64,256]{3,2,1,0:T(8,128)(2,1)} %bitcast.52), calls=%async_computation | async-start | bytes 2097152 | tf_op jit(solution)/shard_map/all_to_all | solution.py:111
  31.4 232.6 %all-reduce.2.cloned.1.call-start = ((), (), s32[]{:S(2)}) async-start(), calls=%async_computation.2 | async-start | bytes 2359296 | tf_op jit(solution)/shard_map/psum | solution.py:77
  31.6 7.4 %copy-start.24 = (bf16[32,256]{1,0:T(8,128)(2,1)S(1)}, bf16[32,256]{1,0:T(8,128)(2,1)}, u32[]{:S(2)}) copy-start(bf16[32,256]{1,0:T(8,128)(2,1)} %param.16) | copy-start | bytes 49156
  32.4 15.2 %collective-permute-start.2 = (bf16[2,256,12,2]{1,3,2,0:T(2,128)(2,1)S(1)}, bf16[2,256,12,2]{1,3,2,0:T(2,128)(2,1)S(1)}, u32[]{:S(2)}, u32[]{:S(2)}) collective-permute-start(bf16[2,256,12,2]{1,3,2,0:T(2,128)(2,1)S(1)} %get-tuple-element.8), channel_id=1, source_target_pairs={{0,1},{1,2},{2,3},{3,4},{4,5},{5,6},{6,7},{7,8},{8,9},{9,10},{10,1... | collective-permute-start | bytes 73736 | tf_op jit(solution)/shard_map/ppermute | solution.py:16
  33.8 13.8 %collective-permute-start.3 = (bf16[2,256,12,2]{1,3,2,0:T(2,128)(2,1)S(1)}, bf16[2,256,12,2]{1,3,2,0:T(2,128)(2,1)S(1)}, u32[]{:S(2)}, u32[]{:S(2)}) collective-permute-start(bf16[2,256,12,2]{1,3,2,0:T(2,128)(2,1)S(1)} %get-tuple-element.9), channel_id=1, source_target_pairs={{1,0},{2,1},{3,2},{4,3},{5,4},{6,5},{7,6},{8,7},{9,8},{10,9},{11,1... | collective-permute-start | bytes 73736 | tf_op jit(solution)/shard_map/ppermute | solution.py:19
  102.5 2.5 copy-start.6
  102.5 3.5 %copy-start.7 = (bf16[8,32,2048]{2,1,0:T(8,128)(2,1)S(1)}, bf16[8,32,2048]{2,1,0:T(8,128)(2,1)}, u32[]{:S(2)}) copy-start(bf16[8,32,2048]{2,1,0:T(8,128)(2,1)} %reshape.151) | copy-start | bytes 3145732
  105.0 2.2 copy-start.8
  106.1 2.2 copy-start.9
  107.1 2.2 copy-start.10
  108.2 2.2 copy-start.11
  109.3 2.2 copy-start.12
  110.4 2.2 copy-start.13
  116.8 5.1 %copy-start.2 = (bf16[256,8,256]{0,2,1:T(8,128)(2,1)S(1)}, bf16[256,8,256]{0,2,1:T(8,128)(2,1)}, u32[]{:S(2)}) copy-start(bf16[256,8,256]{0,2,1:T(8,128)(2,1)} %get-tuple-element.32) | copy-start | bytes 3145732
  126.0 5.1 %copy-start.1 = (bf16[256,8,256]{0,2,1:T(8,128)(2,1)S(1)}, bf16[256,8,256]{0,2,1:T(8,128)(2,1)}, u32[]{:S(2)}) copy-start(bf16[256,8,256]{0,2,1:T(8,128)(2,1)} %get-tuple-element.34) | copy-start | bytes 3145732
  135.3 5.1 %copy-start = (bf16[256,8,256]{0,2,1:T(8,128)(2,1)S(1)}, bf16[256,8,256]{0,2,1:T(8,128)(2,1)}, u32[]{:S(2)}) copy-start(bf16[256,8,256]{0,2,1:T(8,128)(2,1)} %get-tuple-element.36) | copy-start | bytes 3145732
  146.8 2.3 copy-start.3
  147.8 1.3 copy-start.22
  149.1 1.2 copy-start.15
  150.3 1.2 copy-start.16
  151.6 1.2 copy-start.17
  155.3 1.2 copy-start.20
  156.5 1.3 copy-start.21
  156.5 1.4 copy-start.23
  161.2 105.4 %all-to-all-start.1 = ((bf16[16,2,64,256]{3,2,1,0:T(8,128)(2,1)}), bf16[16,2,64,256]{3,2,1,0:T(8,128)(2,1)S(1)}, u32[]{:S(2)}, u32[]{:S(2)}) async-start(bf16[16,2,64,256]{3,2,1,0:T(8,128)(2,1)} %bitcast.15), calls=%async_computation.1 | async-start | bytes 2097152 | tf_op jit(solution)/shard_map/all_to_all | solution.py:122
  168.0 1.8 copy-start.14
  (3 other events, 3.7 us)
Sparse Core Ops, SparseCore 0:
  113.7 150.2 all-reduce.1
where the time goes:
time: 281 us; the launch traced here: 280 us
  local copies, waits for them, and re-layouts  105 us (37%)
  waiting for transfers between devices  99.4 us (35%)
  matrix products  28.2 us (10%)
  starting transfers between devices  26 us (9%)
  between operations  14.5 us (5%)
  other arithmetic  6.43 us (2%)
    psum x1, waiting for transfers between devices, on_device(): weight_grad = lax.psum(local_grad, ('lat', 'lon')) * norm_factor  90.8 us
    slice x10, local copies, waits for them, and re-layouts, on_device(): input_wide[:, 2 * row_tap:2 * row_tap + height, 2 * col_tap:2 * col_tap +...  31 us
    reshape x9, local copies, waits for them, and re-layouts, on_device(): moved_input = moved_input.reshape(groups, group_size, cells)  21 us
    reshape x9, local copies, waits for them, and re-layouts, on_device(): shifted = shifted.reshape(groups, group_size, cells)  18 us
    slice x9, local copies, waits for them, and re-layouts, on_device(): adjoint_wide[:, 4 - 2 * row_tap:4 - 2 * row_tap + height, 4 - 2 * col_tap...  17.4 us
    unnamed x64, local copies, waits for them, and re-layouts  15.5 us
    dot_general x9, matrix products, on_device(): jnp.einsum('gin,gon->gio', moved_input, adjoint_local, preferred_element_...  11 us
    ppermute x2, waiting for transfers between devices, with_halo(): lax.ppermute(lax.slice_in_dim(block, block.shape[dim] - width, None, axis...  8.6 us
  transfers between devices with their start and end apart: 7, of which 2 were waited for; matrix products, arithmetic and copies ran while one was open for 45% of the time, Pallas kernels for 0%

commit v1 on v0

v1 whole, which is shorter than its diff:
```python
import math

import jax
import jax.numpy as jnp
from jax import lax
from jax.experimental import pallas as pl
from jax.experimental.pallas import tpu as pltpu
from jax.sharding import PartitionSpec as P

MESH = pl.DeviceIdType.MESH
N_LAT = 8
N_LON = 16
CH = 256
ROWS = 8
COLS = 256
CELLS = ROWS * COLS
PAD = 16
GROUP = 32
TRACKS = 16
K = 32
PTS = 64
CHUNK = 40
F32 = jnp.float32
BF16 = jnp.bfloat16
NT = (((1,), (1,)), ((), ()))


def iota(shape, dim):
    return lax.broadcasted_iota(jnp.int32, shape, dim)


def kernel(
    owner,
    cell,
    adj_t,
    x_in,
    conv_w,
    obs_w,
    obs_v,
    obs_pc,
    out,
    grad_out,
    ext,
    shifted,
    x_nat,
    x_f32,
    x_mat,
    w_in,
    w_diag,
    blocks,
    obs_op,
    misfit,
    w_buf,
    v_buf,
    pc_buf,
    grad,
    rs_buf,
    part,
    ex_buf,
    gathered,
    local_sem,
    halo_send,
    halo_recv,
    obs_send,
    obs_recv,
    rs_send,
    rs_recv,
    ex_send,
    ex_recv,
    ag_send,
    ag_recv,
):
    lat = lax.axis_index("lat")
    lon = lax.axis_index("lon")
    north = lax.rem(lat + N_LAT - 1, N_LAT)
    south = lax.rem(lat + 1, N_LAT)
    west = lax.rem(lon + N_LON - 1, N_LON)
    east = lax.rem(lon + 1, N_LON)

    local = [
        pltpu.make_async_copy(x_in, x_nat, local_sem.at[0]),
        pltpu.make_async_copy(conv_w, w_in, local_sem.at[1]),
        pltpu.make_async_copy(
            adj_t, ext.at[pl.ds(2, ROWS), pl.ds(PAD, COLS), :], local_sem.at[2]
        ),
        pltpu.make_async_copy(obs_w.at[lon], w_buf.at[lon], local_sem.at[3]),
        pltpu.make_async_copy(obs_v.at[lon], v_buf.at[lon], local_sem.at[4]),
        pltpu.make_async_copy(obs_pc.at[lon], pc_buf.at[lon], local_sem.at[5]),
    ]
    for copy in local:
        copy.start()

    barrier = pltpu.get_barrier_semaphore()

    def greet(to_lat, to_lon):
        pl.semaphore_signal(barrier, inc=1, device_id=(to_lat, to_lon), device_id_type=MESH)

    for to_lat, to_lon in ((north, west), (north, east), (south, west), (south, east)):
        greet(to_lat, to_lon)
    for k in range(1, N_LAT):
        greet(lax.rem(lat + k, N_LAT), lon)
    for k in range(1, N_LON):
        greet(lat, lax.rem(lon + k, N_LON))

    local[0].wait()
    for half in range(2):
        x_f32[half] = (
            x_nat[:, :, 128 * half : 128 * half + 128].astype(F32).reshape(CELLS, 128)
        )
    for i in range(ROWS):
        for half in range(2):
            at = COLS * i + 128 * half
            x_mat[:, at : at + 128] = x_f32[half, pl.ds(i, CH, stride=ROWS), :].astype(BF16)

    pl.semaphore_wait(barrier, 4 + N_LAT - 1 + N_LON - 1)

    def halo(index, rows, cols, to_rows, to_cols, to_lat, to_lon):
        return pltpu.make_async_remote_copy(
            src_ref=adj_t.at[pl.ds(*rows), pl.ds(*cols), :],
            dst_ref=ext.at[pl.ds(*to_rows), pl.ds(*to_cols), :],
            send_sem=halo_send.at[index],
            recv_sem=halo_recv.at[index],
            device_id=(to_lat, to_lon),
            device_id_type=MESH,
        )

    first_rows, last_rows, all_rows = (0, 2), (ROWS - 2, 2), (0, ROWS)
    first_cols, last_cols, all_cols = (0, PAD), (COLS - PAD, PAD), (0, COLS)
    top, bottom, middle = (0, 2), (ROWS + 2, 2), (2, ROWS)
    left, right, centre = (0, PAD), (COLS + PAD, PAD), (PAD, COLS)
    halos = [
        halo(0, all_rows, last_cols, middle, left, lat, east),
        halo(1, all_rows, first_cols, middle, right, lat, west),
        halo(2, last_rows, last_cols, top, left, south, east),
        halo(3, last_rows, first_cols, top, right, south, west),
        halo(4, first_rows, last_cols, bottom, left, north, east),
        halo(5, first_rows, first_cols, bottom, right, north, west),
        halo(6, last_rows, all_cols, top, centre, south, lon),
        halo(7, first_rows, all_cols, bottom, centre, north, lon),
    ]
    for copy in halos:
        copy.start()

    def obs_copies(k):
        peer = lax.rem(lon + k, N_LON)
        return [
            pltpu.make_async_remote_copy(
                src_ref=src.at[peer],
                dst_ref=dst.at[lon],
                send_sem=obs_send.at[index, k],
                recv_sem=obs_recv.at[index, k],
                device_id=(lat, peer),
                device_id_type=MESH,
            )
            for index, (src, dst) in enumerate(
                ((obs_w, w_buf), (obs_v, v_buf), (obs_pc, pc_buf))
            )
        ]

    def start_obs(k, carry):
        for copy in obs_copies(k):
            copy.start()
        return carry

    lax.fori_loop(1, N_LON, start_obs, 0)

    local[1].wait()
    spread = (iota((CH, GROUP), 0) % GROUP == iota((CH, GROUP), 1)).astype(F32).astype(BF16)
    same_group = iota((CH, CH), 0) // GROUP == iota((CH, CH), 1) // GROUP
    for tap in range(9):
        stacked = jnp.concatenate([w_in[g, tap] for g in range(CH // GROUP)], axis=0)
        tiled = lax.dot_general(spread, stacked, NT, preferred_element_type=F32)
        w_diag[tap] = jnp.where(same_group, tiled, 0.0).astype(BF16)

    local[2].wait()
    scale = 1.0 / math.sqrt(CELLS * N_LAT * N_LON)
    lane_group = iota((GROUP, 128), 1) // GROUP

    def add_grad(tap, x_from, rows, read, fresh):
        product = jnp.dot(
            x_mat[:, COLS * x_from : COLS * (x_from + rows)],
            read.reshape(rows * COLS, CH),
            preferred_element_type=F32,
        )
        for half in range(2):
            value = jnp.zeros((GROUP, 128), F32)
            for q in range(4):
                g = 4 * half + q
                block = product[g * GROUP : (g + 1) * GROUP, 128 * half : 128 * half + 128]
                value = jnp.where(lane_group == q, block, value)
            value = value * scale
            at = pl.ds(tap * 64 + half * GROUP, GROUP)
            grad[at, :] = value if fresh else grad[at, :] + value

    inner = ((0, 0, 6, 4), (1, 0, 8, 2), (2, 2, 6, 2))
    for a, x_from, rows, row in inner:
        add_grad(
            3 * a + 1, x_from, rows, ext[row : row + rows, PAD : PAD + COLS, :], True
        )

    def shift_row(row):
        shifted[0, row] = ext[row, pl.ds(PAD + 2, COLS), :]
        shifted[1, row] = ext[row, pl.ds(PAD - 2, COLS), :]

    halos[0].wait_recv()
    halos[1].wait_recv()

    def shift_inner(row, carry):
        shift_row(row)
        return carry

    lax.fori_loop(2, ROWS + 2, shift_inner, 0)
    for a, x_from, rows, row in inner:
        for b in (0, 2):
            add_grad(3 * a + b, x_from, rows, shifted[b // 2, row : row + rows], True)

    for copy in halos[2:]:
        copy.wait_recv()

    @pl.when(lat == 0)
    def _():
        ext[0:2] = jnp.zeros((2, COLS + 2 * PAD, CH), BF16)

    @pl.when(lat == N_LAT - 1)
    def _():
        ext[ROWS + 2 : ROWS + 4] = jnp.zeros((2, COLS + 2 * PAD, CH), BF16)

    for row in (0, 1, ROWS + 2, ROWS + 3):
        shift_row(row)
    for a, x_from, row in ((0, 6, 10), (2, 0, 0)):
        add_grad(3 * a + 1, x_from, 2, ext[row : row + 2, PAD : PAD + COLS, :], False)
        for b in (0, 2):
            add_grad(3 * a + b, x_from, 2, shifted[b // 2, row : row + 2], False)
    grad[576:640, :] = jnp.zeros((64, 128), F32)

    def rs_copy(k):
        peer = lax.rem(lon + k, N_LON)
        return pltpu.make_async_remote_copy(
            src_ref=grad.at[pl.ds(pl.multiple_of(CHUNK * peer, 8), CHUNK), :],
            dst_ref=rs_buf.at[k],
            send_sem=rs_send.at[k],
            recv_sem=rs_recv.at[k],
            device_id=(lat, peer),
            device_id_type=MESH,
        )

    def start_rs(k, carry):
        rs_copy(k).start()
        return carry

    lax.fori_loop(1, N_LON, start_rs, 0)

    for copy in local[3:]:
        copy.wait()

    def wait_obs(k, carry):
        for copy in obs_copies(k):
            copy.wait_recv()
        return carry

    lax.fori_loop(1, N_LON, wait_obs, 0)
    owners = [owner[t] for t in range(TRACKS)]
    places = [
        jnp.minimum(
            sum([(owners[u] == owners[t]).astype(jnp.int32) for u in range(t)], jnp.int32(0)), 1
        )
        for t in range(TRACKS)
    ]
    widen = (iota((PTS, 4 * PTS), 1) % PTS == iota((PTS, 4 * PTS), 0)).astype(F32).astype(BF16)
    same_track = iota((4 * K, 4 * PTS), 0) // K == iota((4 * K, 4 * PTS), 1) // PTS
    obs_row = iota((K, PTS), 0).astype(F32)
    for q in range(4):
        picked = []
        for t in range(4 * q, 4 * q + 4):
            weight = w_buf[owners[t], places[t]]
            count = pc_buf[owners[t], places[t]][1:2, :PTS].astype(F32)
            picked.append(jnp.where(obs_row < count, weight.astype(F32), 0.0))
        stacked = jnp.concatenate(picked, axis=0).astype(BF16)
        tiled = jnp.dot(stacked, widen, preferred_element_type=F32)
        blocks[q] = jnp.where(same_track, tiled, 0.0).astype(BF16)

    def build_op(i, carry):
        here = iota((COLS, 4 * PTS), 0) + i * COLS
        at = pl.ds(pl.multiple_of(i * COLS, COLS), COLS)
        for q in range(4):
            hit = jnp.where(here == cell[q : q + 1, :], 1.0, 0.0).astype(BF16)
            obs_op[at, 4 * K * q : 4 * K * (q + 1)] = lax.dot_general(
                hit, blocks[q], NT, preferred_element_type=F32
            ).astype(BF16)
        return carry

    lax.fori_loop(0, ROWS, build_op, 0)
    model_obs = jnp.dot(x_mat[...], obs_op[...], preferred_element_type=F32).T
    for t in range(TRACKS):
        at = slice(K * t, K * (t + 1))
        value = v_buf[owners[t], places[t]].astype(F32)
        precision = pc_buf[owners[t], places[t]][0:1, :].astype(F32)
        misfit[at, :] = ((model_obs[at, :] - value) * precision).astype(BF16)

    def finish_rows(first, last):
        def one(i, carry):
            total = ext[i + 2, PAD : PAD + COLS, :].astype(F32)
            for a in range(3):
                row = i + 4 - 2 * a
                taps = (
                    shifted[0, row],
                    ext[row, PAD : PAD + COLS, :],
                    shifted[1, row],
                )
                for b in range(3):
                    total += jnp.dot(
                        taps[b], w_diag[3 * a + b], preferred_element_type=F32
                    )
            at = pl.ds(pl.multiple_of(i * COLS, COLS), COLS)
            total += jnp.dot(obs_op[at, :], misfit[...], preferred_element_type=F32)
            out[i] = total.astype(BF16)
            return carry

        lax.fori_loop(first, last, one, 0)

    def wait_rs(k, carry):
        rs_copy(k).wait_recv()
        return carry

    lax.fori_loop(1, N_LON, wait_rs, 0)
    own = grad[pl.ds(pl.multiple_of(CHUNK * lon, 8), CHUNK), :]
    for k in range(1, N_LON):
        own += rs_buf[k]
    part[...] = own
    ex_buf[lat] = own

    def ex_copy(k):
        return pltpu.make_async_remote_copy(
            src_ref=part,
            dst_ref=ex_buf.at[lat],
            send_sem=ex_send.at[k],
            recv_sem=ex_recv.at[k],
            device_id=(lax.rem(lat + k, N_LAT), lon),
            device_id_type=MESH,
        )

    for k in range(1, N_LAT):
        ex_copy(k).start()
    finish_rows(0, 4)
    for k in range(1, N_LAT):
        ex_copy(k).wait_recv()
    whole = ex_buf[0]
    for k in range(1, N_LAT):
        whole += ex_buf[k]
    mine = pl.ds(pl.multiple_of(CHUNK * lon, 8), CHUNK)
    gathered[mine, :] = whole

    def ag_copy(k):
        return pltpu.make_async_remote_copy(
            src_ref=gathered.at[mine, :],
            dst_ref=gathered.at[mine, :],
            send_sem=ag_send.at[k],
            recv_sem=ag_recv.at[k],
            device_id=(lat, lax.rem(lon + k, N_LON)),
            device_id_type=MESH,
        )

    def start_ag(k, carry):
        ag_copy(k).start()
        return carry

    lax.fori_loop(1, N_LON, start_ag, 0)
    finish_rows(4, 8)

    def wait_ag(k, carry):
        ag_copy(k).wait_recv()
        return carry

    lax.fori_loop(1, N_LON, wait_ag, 0)
    grad_out[...] = gathered[0:576, :]

    for copy in halos:
        copy.wait_send()

    def wait_sends(k, carry):
        for copy in obs_copies(k):
            copy.wait_send()
        rs_copy(k).wait_send()
        ag_copy(k).wait_send()
        return carry

    lax.fori_loop(1, N_LON, wait_sends, 0)
    for k in range(1, N_LAT):
        ex_copy(k).wait_send()


def on_device(
    adjoint_in,
    layer_input,
    conv_weight,
    footprint,
    owner,
    obs_weight,
    obs_value,
    obs_precision,
    obs_count,
):
    lat_start = lax.axis_index("lat") * ROWS
    lon_start = lax.axis_index("lon") * COLS
    full_width = COLS * N_LON
    cell = (footprint // full_width - lat_start) * COLS + (footprint % full_width - lon_start)
    counts = jnp.broadcast_to(obs_count[:, None], (2 * N_LON, CH)).astype(BF16)
    precision_count = jnp.stack([obs_precision, counts], axis=1).reshape(N_LON, 2, 2, CH)
    anywhere = pl.BlockSpec(memory_space=pl.ANY)
    vmem = pl.BlockSpec(memory_space=pltpu.VMEM)
    out, grad = pl.pallas_call(
        kernel,
        out_shape=(
            jax.ShapeDtypeStruct((ROWS, COLS, CH), BF16),
            jax.ShapeDtypeStruct((576, 128), F32),
        ),
        in_specs=[pl.BlockSpec(memory_space=pltpu.SMEM), vmem] + [anywhere] * 6,
        out_specs=(vmem, vmem),
        scratch_shapes=[
            pltpu.VMEM((ROWS + 4, COLS + 2 * PAD, CH), BF16),
            pltpu.VMEM((2, ROWS + 4, COLS, CH), BF16),
            pltpu.VMEM((CH, ROWS, COLS), BF16),
            pltpu.VMEM((2, CELLS, 128), F32),
            pltpu.VMEM((CH, CELLS), BF16),
            pltpu.VMEM((CH // GROUP, 9, GROUP, GROUP), BF16),
            pltpu.VMEM((9, CH, CH), BF16),
            pltpu.VMEM((4, 4 * K, 4 * PTS), BF16),
            pltpu.VMEM((CELLS, TRACKS * K), BF16),
            pltpu.VMEM((TRACKS * K, CH), BF16),
            pltpu.VMEM((N_LON, 2, K, PTS), BF16),
            pltpu.VMEM((N_LON, 2, K, CH), BF16),
            pltpu.VMEM((N_LON, 2, 2, CH), BF16),
            pltpu.VMEM((640, 128), F32),
            pltpu.VMEM((N_LON, CHUNK, 128), F32),
            pltpu.VMEM((CHUNK, 128), F32),
            pltpu.VMEM((N_LAT, CHUNK, 128), F32),
            pltpu.VMEM((640, 128), F32),
            pltpu.SemaphoreType.DMA((6,)),
            pltpu.SemaphoreType.DMA((8,)),
            pltpu.SemaphoreType.DMA((8,)),
            pltpu.SemaphoreType.DMA((3, N_LON)),
            pltpu.SemaphoreType.DMA((3, N_LON)),
            pltpu.SemaphoreType.DMA((N_LON,)),
            pltpu.SemaphoreType.DMA((N_LON,)),
            pltpu.SemaphoreType.DMA((N_LAT,)),
            pltpu.SemaphoreType.DMA((N_LAT,)),
            pltpu.SemaphoreType.DMA((N_LON,)),
            pltpu.SemaphoreType.DMA((N_LON,)),
        ],
        compiler_params=pltpu.CompilerParams(
            collective_id=0, has_side_effects=True, vmem_limit_bytes=50 * 1024 * 1024
        ),
    )(
        owner.reshape(TRACKS),
        cell.reshape(4, 4 * PTS),
        jnp.transpose(adjoint_in, (1, 2, 0)),
        layer_input,
        conv_weight,
        obs_weight.reshape(N_LON, 2, K, PTS),
        obs_value.reshape(N_LON, 2, K, CH),
        precision_count,
    )
    weight_grad = grad.reshape(9, 2, GROUP, 4, GROUP).transpose(1, 3, 0, 2, 4)
    return (
        jnp.transpose(out, (2, 0, 1)),
        weight_grad.reshape(CH // GROUP, 9, GROUP, GROUP),
    )


def solution(mesh):
    in_specs = (
        P(None, "lat", "lon"),
        P(None, "lat", "lon"),
        P(),
        P(("lat", "lon"), None),
        P(("lat", "lon"), None),
        P(("lat", "lon"), None, None),
        P(("lat", "lon"), None, None),
        P(("lat", "lon"), None),
        P(("lat", "lon")),
    )
    out_specs = (P(None, "lat", "lon"), P())
    return jax.shard_map(
        on_device, mesh=mesh, in_specs=in_specs, out_specs=out_specs, check_vma=False
    )
```

time: 281 us -> 50.5 us (0.18)
  waiting for transfers between devices: 99.4 us -> 0 us
  local copies, waits for them, and re-layouts: 105 us -> 7.05 us
  Pallas kernels: 0 us -> 40.7 us
  matrix products: 28.2 us -> 0 us
  starting transfers between devices: 26 us -> 0 us
  between operations: 14.5 us -> 0.73 us
  other arithmetic: 6.43 us -> 1.55 us
    psum x1 -> x0, waiting for transfers between devices: 90.8 us -> none  [on_device(): weight_grad = lax.psum(local_grad, ('lat', 'lon')) * norm_factor]
    slice x19 -> x0, local copies, waits for them, and re-layouts: 48.4 us -> none  [the longest x10 31 us: on_device(): input_wide[:, 2 * row_tap:2 * row_tap + height, 2 * col_tap:2 * col_tap +...]
    pallas_call x0 -> x1, Pallas kernels: none -> 40.7 us  [on_device(): pl.pallas_call(kernel, out_shape=(jax.ShapeDtypeStruct((ROWS, COLS, CH),...]
    reshape x20 -> x2, local copies, waits for them, and re-layouts: 40.8 us -> 0.58 us  [the longest x1 0.5 us: on_device(): weight_grad = grad.reshape(9, 2, GROUP, 4, GROUP).transpose(1, 3, 0, 2, 4)]
    dot_general x23 -> x0, matrix products: 28.2 us -> none  [the longest x9 11 us: on_device(): jnp.einsum('gin,gon->gio', moved_input, adjoint_local, preferred_element_...]
    all_to_all x2 -> x0, starting transfers between devices: 14.6 us -> none  [the longest x1 7.82 us: on_device(): lax.all_to_all(outgoing, 'lon', split_axis=0, concat_axis=0, tiled=True)]
    ppermute x4 -> x0, starting transfers between devices: 11.4 us -> none  [the longest x2 5.88 us: with_halo(): lax.ppermute(lax.slice_in_dim(block, block.shape[dim] - width, None, axis...]
    unnamed x64 -> x10, local copies, waits for them, and re-layouts: 15.5 us -> 4.38 us
  transfers between devices with their start and end apart: 7 -> 0, of which waited for: 2 -> 0; matrix products, arithmetic and copies ran while one was open for 45% -> 0% of each run, Pallas kernels for 0% -> 0%
where the time goes in v1:
time: 50.5 us; the launch traced here: 50.1 us
  Pallas kernels  40.7 us (81%)
  local copies, waits for them, and re-layouts  7.05 us (14%)
  other arithmetic  1.55 us (3%)
  between operations  0.73 us (1%)
    pallas_call x1, Pallas kernels, on_device(): pl.pallas_call(kernel, out_shape=(jax.ShapeDtypeStruct((ROWS, COLS, CH),...  40.7 us
    unnamed x10, local copies, waits for them, and re-layouts  4.38 us
    transpose x1, local copies, waits for them, and re-layouts, on_device(): weight_grad = grad.reshape(9, 2, GROUP, 4, GROUP).transpose(1, 3, 0, 2, 4)  1.17 us

profile of v1, /device:TPU:1, one launch (start us, length us, event | category | flops | bytes accessed | tf_op | source)
XLA Modules:
  0.0 50.1 jit_solution(8737849817039395685)
XLA Ops:
  0.6 0.0 copy-start.1
  0.6 0.0 copy-start.3
  0.7 0.0 copy-start
  0.7 0.7 %convert_element_type.4 = bf16[32]{0:T(256)(128)(2,1)S(1)} convert(s32[32]{0:T(128)} %param.17) | non-fusion elementwise | flops 32 | bytes 192 | tf_op jit(solution)/shard_map/convert_element_type | solution.py:407
  1.4 0.1 stack.12
  1.5 0.7 %fusion.2 = s32[16,64]{1,0:T(8,128)S(1)} fusion(s32[16,64]{1,0:T(8,128)} %param.12, s32[]{:T(128)S(6)} %mul.15, s32[]{:T(128)S(6)} %mul.12), kind=kLoop, calls=%fused_computation.8 | loop fusion | flops 23552 | bytes 8200 | tf_op jit(solution)/shard_map/add | solution.py:406
  2.2 0.1 reshape.29.cell
  2.3 0.1 stack.13
  2.4 0.7 %stack.15 = bf16[16,2,1,256]{3,2,1,0:T(2,128)(2,1)S(1)} reshape(bf16[32,256]{1,0:T(8,128)(2,1)} %param.16) | data formatting | bytes 32768 | tf_op jit(solution)/shard_map/stack | solution.py:408
  3.1 0.1 pad_maximum_fusion.obs_pc
  3.2 1.6 %copy.14 = bf16[256,8,256]{0,2,1:T(8,128)(2,1)S(1)} copy(bf16[256,8,256]{2,1,0:T(8,128)(2,1)} %param.9) | data formatting | bytes 2097152 | tf_op args[0]
  4.9 0.0 copy-done.1
  4.9 0.0 copy-done.3
  4.9 0.0 copy-done
  4.9 0.0 copy-start.2
  4.9 0.9 %copy-done.2 = bf16[32,32,64]{2,1,0:T(8,128)(2,1)S(1)} copy-done((bf16[32,32,64]{2,1,0:T(8,128)(2,1)S(1)}, bf16[32,32,64]{2,1,0:T(8,128)(2,1)}, u32[]{:S(2)}) %copy-start.2) | copy-done | bytes 131096
  5.8 40.7 %shard_map.104 = (bf16[8,256,256]{2,1,0:T(8,128)(2,1)S(1)}, f32[576,128]{1,0:T(8,128)S(1)}) custom-call(s32[16]{0:T(128)S(1)} %bitcast.11, s32[4,256]{1,0:T(4,128)S(1)} %reshape.29.cell, bf16[8,256,256]{2,1,0:T(8,128)(2,1)S(1)} %bitcast.7, bf16[256,8,256]{2,1,0:T(8,128)(2,1)} %x_in.1, bf16[8,9,32,32]{3,2,1,0:T(8,128)(2,1)S(1)} %copy-done, ...), custom_call_target="tpu_custom_call" | custom-call | tf_op jit(solution)/shard_map/pallas_call | solution.py:411
  46.6 1.8 %copy.17 = bf16[256,8,256]{2,1,0:T(8,128)(2,1)} copy(bf16[256,8,256]{0,2,1:T(8,128)(2,1)S(1)} %bitcast.8) | data formatting | bytes 2097152
  48.4 0.5 %reshape.32 = f32[9,2,32,4,32]{4,3,2,1,0:T(4,128)S(1)} reshape(f32[576,128]{1,0:T(8,128)S(1)} %get-tuple-element.5) | data formatting | bytes 589824 | tf_op jit(solution)/shard_map/reshape | solution.py:463
  48.9 1.2 %copy.16 = f32[2,4,9,32,32]{4,3,2,1,0:T(8,128)} copy(f32[2,4,9,32,32]{4,1,3,0,2:T(4,128)S(1)} %bitcast.12) | data formatting | bytes 589824 | tf_op jit(solution)/shard_map/transpose | solution.py:463
Async XLA Ops:
  0.6 4.2 %copy-start.1 = (bf16[32,32,256]{2,1,0:T(8,128)(2,1)S(1)}, bf16[32,32,256]{2,1,0:T(8,128)(2,1)}, u32[]{:S(2)}) copy-start(bf16[32,32,256]{2,1,0:T(8,128)(2,1)} %param.15) | copy-start | bytes 1572868
  0.6 4.2 %copy-start.3 = (s32[16,1]{0,1:T(1,128)S(1)}, s32[16,1]{0,1:T(1,128)}, u32[]{:S(2)}) copy-start(s32[16,1]{0,1:T(1,128)} %param.13) | copy-start | bytes 196
  0.7 4.2 %copy-start = (bf16[8,9,32,32]{3,2,1,0:T(8,128)(2,1)S(1)}, bf16[8,9,32,32]{3,2,1,0:T(8,128)(2,1)}, u32[]{:S(2)}) copy-start(bf16[8,9,32,32]{3,2,1,0:T(8,128)(2,1)} %conv_w.1) | copy-start | bytes 442372
  4.9 1.0 %copy-start.2 = (bf16[32,32,64]{2,1,0:T(8,128)(2,1)S(1)}, bf16[32,32,64]{2,1,0:T(8,128)(2,1)}, u32[]{:S(2)}) copy-start(bf16[32,32,64]{2,1,0:T(8,128)(2,1)} %param.14) | copy-start | bytes 393220

commit v2 on v1

v2 whole, which is shorter than its diff:
```python
import math

import jax
import jax.numpy as jnp
from jax import lax
from jax.experimental import pallas as pl
from jax.experimental.pallas import tpu as pltpu
from jax.sharding import PartitionSpec as P

MESH = pl.DeviceIdType.MESH
N_LAT = 8
N_LON = 16
CH = 256
ROWS = 8
COLS = 256
CELLS = ROWS * COLS
GROUP = 32
TRACKS = 16
K = 32
PTS = 64
CHUNK = 40
CB = 64
F32 = jnp.float32
BF16 = jnp.bfloat16
NT = (((1,), (1,)), ((), ()))


def iota(shape, dim):
    return lax.broadcasted_iota(jnp.int32, shape, dim)


def turn(value, shift):
    return pltpu.roll(value, shift % 128, 1) if shift % 128 else value


def kernel(
    owner_in,
    counts_in,
    fp_in,
    adj_in,
    x_in,
    conv_w,
    obs_w,
    obs_v,
    obs_p,
    out,
    grad_out,
    owner,
    counts,
    fp,
    a_nat,
    x_nat,
    f_buf,
    a_rows,
    a_shift,
    x_rows,
    x_edge,
    e_own,
    e_in,
    e_wide,
    halo_cols,
    a_edge,
    w_in,
    w_diag,
    obs_op,
    blocks,
    cell_row,
    w_nat,
    p_nat,
    w_own,
    p_own,
    w_buf,
    v_buf,
    p_buf,
    grad,
    g_acc,
    rs_buf,
    part,
    ex_buf,
    gathered,
    local_sem,
    halo_send,
    halo_recv,
    obs_send,
    obs_recv,
    rs_send,
    rs_recv,
    ex_send,
    ex_recv,
    ag_send,
    ag_recv,
):
    lat = lax.axis_index("lat")
    lon = lax.axis_index("lon")
    north = lax.rem(lat + N_LAT - 1, N_LAT)
    south = lax.rem(lat + 1, N_LAT)
    west = lax.rem(lon + N_LON - 1, N_LON)
    east = lax.rem(lon + 1, N_LON)

    local = [
        pltpu.make_async_copy(src, dst, local_sem.at[index])
        for index, (src, dst) in enumerate(
            (
                (adj_in, a_nat),
                (x_in, x_nat),
                (obs_w, w_nat),
                (obs_p, p_nat),
                (conv_w, w_in),
                (obs_v.at[lon], v_buf.at[lon]),
                (owner_in, owner),
                (counts_in, counts),
                (fp_in, fp),
            )
        )
    ]
    for copy in local:
        copy.start()

    barrier = pltpu.get_barrier_semaphore()

    def greet(to_lat, to_lon):
        pl.semaphore_signal(barrier, inc=1, device_id=(to_lat, to_lon), device_id_type=MESH)

    for to_lat, to_lon in ((north, west), (north, east), (south, west), (south, east)):
        greet(to_lat, to_lon)
    for k in range(1, N_LAT):
        greet(lax.rem(lat + k, N_LAT), lon)
    for k in range(1, N_LON):
        greet(lat, lax.rem(lon + k, N_LON))

    lane = iota((CB, 128), 1)

    def split_rows(native, put):
        for half in range(2):
            f_buf[half] = (
                native[:, :, 128 * half : 128 * half + 128].astype(F32).reshape(CELLS, 128)
            )
        for c in range(0, CH, CB):
            first = jnp.zeros((CB, 128), F32)
            last = jnp.zeros((CB, 128), F32)
            for i in range(ROWS):
                low = f_buf[0, pl.ds(ROWS * c + i, CB, stride=ROWS), :]
                high = f_buf[1, pl.ds(ROWS * c + i, CB, stride=ROWS), :]
                here = lane // 2 == i
                first = jnp.where(here, turn(low, 2 * i), first)
                last = jnp.where(here, turn(high, 2 * i + 2), last)
                put(i, c, low, high)
            yield c, first, last

    local[0].wait()

    def put_adjoint(i, c, low, high):
        a_rows[i + 2, c : c + CB, :128] = low.astype(BF16)
        a_rows[i + 2, c : c + CB, 128:] = high.astype(BF16)

    for c, first, last in split_rows(a_nat, put_adjoint):
        halo_cols[0, c : c + CB, :] = first
        halo_cols[1, c : c + CB, :] = last
    for side in range(2):
        e_own[side] = halo_cols[side].T[: 2 * ROWS, :].astype(BF16)

    local[2].wait()
    local[3].wait()
    local[7].wait()
    obs_row = iota((K, PTS), 0)
    for s in range(2 * N_LON):
        w_own[s // 2, :, PTS * (s % 2) : PTS * (s % 2 + 1)] = jnp.where(
            obs_row < counts[s], w_nat[s].astype(F32), 0.0
        ).astype(BF16)
    for s in range(N_LON):
        p_own[s] = p_nat[2 * s : 2 * s + 2, :]
    w_buf[lon] = w_own[lon]
    p_buf[lon] = p_own[lon]

    local[1].wait()

    def put_input(i, c, low, high):
        at = slice(c, c + CB)
        low_back, high_back = turn(low, 2), turn(high, 2)
        low_on, high_on = turn(low, -2), turn(high, -2)
        x_rows[0, i, at, :128] = jnp.where(lane < 2, 0.0, low_back).astype(BF16)
        x_rows[0, i, at, 128:] = jnp.where(lane < 2, low_back, high_back).astype(BF16)
        x_rows[1, i, at, :128] = low.astype(BF16)
        x_rows[1, i, at, 128:] = high.astype(BF16)
        x_rows[2, i, at, :128] = jnp.where(lane < 126, low_on, high_on).astype(BF16)
        x_rows[2, i, at, 128:] = jnp.where(lane < 126, high_on, 0.0).astype(BF16)

    for c, first, last in split_rows(x_nat, put_input):
        x_edge[0, c : c + CB, :] = last.astype(BF16)
        x_edge[1, c : c + CB, :] = turn(first, 64).astype(BF16)

    groups = CH // GROUP

    def meeting(g, rows):
        at = slice(GROUP * g, GROUP * (g + 1))
        moved = [
            jnp.concatenate([x_rows[b, i, at, :] for b in range(3)], axis=0) for i in rows
        ]
        meets = [
            jnp.concatenate([a_rows[i + 4 - 2 * a, at, :] for a in (0, 1, 2, 2)], axis=0)
            for i in rows
        ]
        return moved, meets

    def pair_up(moved, meets):
        return lax.dot_general(
            jnp.concatenate(moved, axis=1),
            jnp.concatenate(meets, axis=1),
            NT,
            preferred_element_type=F32,
        )

    for g in range(groups):
        g_acc[g] = pair_up(*meeting(g, range(2, ROWS - 2)))

    local[4].wait()
    spread = (iota((GROUP, CH), 1) % GROUP == iota((GROUP, CH), 0)).astype(F32).astype(BF16)
    same_group = iota((CH, CH), 0) // GROUP == iota((CH, CH), 1) // GROUP
    for tap in range(9):
        stacked = jnp.concatenate([w_in[g, tap] for g in range(groups)], axis=0)
        tiled = jnp.dot(stacked, spread, preferred_element_type=F32)
        w_diag[:, CH * tap : CH * (tap + 1)] = jnp.where(same_group, tiled, 0.0).astype(BF16)

    pl.semaphore_wait(barrier, 4 + N_LAT - 1 + N_LON - 1)

    def halo(index, src, dst, to_lat, to_lon):
        return pltpu.make_async_remote_copy(
            src_ref=src,
            dst_ref=dst,
            send_sem=halo_send.at[index],
            recv_sem=halo_recv.at[index],
            device_id=(to_lat, to_lon),
            device_id_type=MESH,
        )

    halos = [
        halo(0, e_own.at[1], e_in.at[0], lat, east),
        halo(1, e_own.at[0], e_in.at[1], lat, west),
        halo(2, e_own.at[1], e_in.at[2], south, east),
        halo(3, e_own.at[0], e_in.at[3], south, west),
        halo(4, e_own.at[1], e_in.at[4], north, east),
        halo(5, e_own.at[0], e_in.at[5], north, west),
    ]
    for part_of in range(2):
        at = pl.ds(CH // 2 * part_of, CH // 2)
        for src, dst, to_lat in ((ROWS, 0, south), (2, ROWS + 2, north)):
            halos.append(
                halo(
                    len(halos),
                    a_rows.at[pl.ds(src, 2), at],
                    a_rows.at[pl.ds(dst, 2), at],
                    to_lat,
                    lon,
                )
            )
    for copy in halos:
        copy.start()

    def obs_copies(k):
        peer = lax.rem(lon + k, N_LON)
        return [
            pltpu.make_async_remote_copy(
                src_ref=src.at[peer],
                dst_ref=dst.at[lon],
                send_sem=obs_send.at[index, k],
                recv_sem=obs_recv.at[index, k],
                device_id=(lat, peer),
                device_id_type=MESH,
            )
            for index, (src, dst) in enumerate(
                ((w_own, w_buf), (obs_v, v_buf), (p_own, p_buf))
            )
        ]

    def start_obs(k, carry):
        for copy in obs_copies(k):
            copy.start()
        return carry

    lax.fori_loop(1, N_LON, start_obs, 0)

    for copy in halos[:6]:
        copy.wait_recv()

    wide_lane = iota((CH, 128), 1)
    for side in range(2):
        upper = e_in[2 + side].astype(F32)[2 * ROWS - 4 :, :]
        lower = e_in[4 + side].astype(F32)[:4, :]
        e_wide[0:4, :] = jnp.where(lat > 0, upper, 0.0)
        e_wide[4 : 4 + 2 * ROWS, :] = e_in[side].astype(F32)
        e_wide[4 + 2 * ROWS : 8 + 2 * ROWS, :] = jnp.where(lat < N_LAT - 1, lower, 0.0)
        e_wide[8 + 2 * ROWS :, :] = jnp.zeros((120 - 2 * ROWS, CH), F32)
        halo_cols[side] = e_wide[...].T
    for a in range(3):
        from_east = turn(halo_cols[1], 4 * a - 8)
        from_west = turn(halo_cols[0], 64 + 4 * a - 8)
        a_edge[a] = jnp.where(wide_lane < 64, from_east, from_west).astype(BF16)

    scale = 1.0 / math.sqrt(CELLS * N_LAT * N_LON)
    nothing = jnp.zeros((GROUP, 128), BF16)
    tile_lane = iota((3 * GROUP, 128), 1)
    done = []
    for g in range(groups):
        if g % 4 == 0:
            half = pl.ds(CH // 2 * (g // 4), CH // 2)
            for copy in halos[6 + g // 2 : 8 + g // 2]:
                copy.wait_recv()

            @pl.when(lat == 0)
            def _(half=half):
                a_rows[0:2, half] = jnp.zeros((2, CH // 2, COLS), BF16)

            @pl.when(lat == N_LAT - 1)
            def _(half=half):
                a_rows[ROWS + 2 : ROWS + 4, half] = jnp.zeros((2, CH // 2, COLS), BF16)

        at = slice(GROUP * g, GROUP * (g + 1))
        moved, meets = meeting(g, (0, 1, ROWS - 2, ROWS - 1))
        moved.append(jnp.concatenate([x_edge[0, at, :], nothing, x_edge[1, at, :]], axis=0))
        meets.append(jnp.concatenate([a_edge[a, at, :] for a in (0, 1, 2, 2)], axis=0))
        total = (pair_up(moved, meets) + g_acc[g]) * scale
        done.append(total)
        if g % 2 == 1:
            at = 96 * (g // 2)
            grad[at : at + 96, :] = jnp.where(tile_lane < 64, done[g - 1], turn(total, 64))
        if g % 4 == 3:
            value = turn(done[g - 3], -64)
            for m in range(1, 4):
                shifted = turn(done[g - 3 + m], 32 * m - 64)
                value = jnp.where(tile_lane // GROUP == m, shifted, value)
            at = 384 + 96 * (g // 4)
            grad[at : at + 96, :] = value
    grad[576:640, :] = jnp.zeros((64, 128), F32)

    def rs_copy(k):
        peer = lax.rem(lon + k, N_LON)
        return pltpu.make_async_remote_copy(
            src_ref=grad.at[pl.ds(pl.multiple_of(CHUNK * peer, 8), CHUNK), :],
            dst_ref=rs_buf.at[k],
            send_sem=rs_send.at[k],
            recv_sem=rs_recv.at[k],
            device_id=(lat, peer),
            device_id_type=MESH,
        )

    def start_rs(k, carry):
        rs_copy(k).start()
        return carry

    lax.fori_loop(1, N_LON, start_rs, 0)

    for row in range(ROWS + 4):
        for c in range(0, CH, CB):
            at = slice(c, c + CB)
            low = a_rows[row, at, :128].astype(F32)
            high = a_rows[row, at, 128:].astype(F32)
            low_on, high_on = turn(low, -2), turn(high, -2)
            low_back, high_back = turn(low, 2), turn(high, 2)
            east_cols = turn(halo_cols[1, at, :], 126 - 2 * row)
            west_cols = turn(halo_cols[0, at, :], -2 * row)
            a_shift[0, row, at, :128] = jnp.where(lane < 126, low_on, high_on).astype(BF16)
            a_shift[0, row, at, 128:] = jnp.where(lane < 126, high_on, east_cols).astype(BF16)
            a_shift[1, row, at, :128] = jnp.where(lane < 2, west_cols, low_back).astype(BF16)
            a_shift[1, row, at, 128:] = jnp.where(lane < 2, low_back, high_back).astype(BF16)

    for copy in (local[5], local[6], local[8]):
        copy.wait()

    def wait_obs(k, carry):
        for copy in obs_copies(k):
            copy.wait_recv()
        return carry

    lax.fori_loop(1, N_LON, wait_obs, 0)
    owners = [owner[t] for t in range(TRACKS)]
    places = [
        jnp.minimum(
            sum([(owners[u] == owners[t]).astype(jnp.int32) for u in range(t)], jnp.int32(0)), 1
        )
        for t in range(TRACKS)
    ]
    cells = fp[...]
    width = COLS * N_LON
    rows_of = (cells // width - lat * ROWS).astype(F32).astype(BF16)
    cols_of = (cells % width - lon * COLS).astype(F32).astype(BF16)
    widen = (iota((PTS, 4 * PTS), 1) % PTS == iota((PTS, 4 * PTS), 0)).astype(F32).astype(BF16)
    cell = COLS * jnp.dot(rows_of, widen, preferred_element_type=F32) + jnp.dot(
        cols_of, widen, preferred_element_type=F32
    )
    widen_pair = jnp.concatenate([widen, widen], axis=0)
    slot_lane = iota((K, 2 * PTS), 1) // PTS
    own_lanes = iota((TRACKS, 4 * PTS), 1) // PTS == iota((TRACKS, 4 * PTS), 0) % 4
    cell = jnp.where(own_lanes, cell, 0.0)
    same_track = iota((4 * K, 4 * PTS), 0) // K == iota((4 * K, 4 * PTS), 1) // PTS
    for q in range(4):
        tracks = range(4 * q, 4 * q + 4)
        stacked = jnp.concatenate(
            [jnp.where(slot_lane == places[t], w_buf[owners[t]].astype(F32), 0.0) for t in tracks],
            axis=0,
        )
        tiled = jnp.dot(stacked.astype(BF16), widen_pair, preferred_element_type=F32)
        blocks[q] = jnp.where(same_track, tiled, 0.0).astype(BF16)
        cell_row[q : q + 1, :] = jnp.sum(cell[4 * q : 4 * q + 4, :], axis=0, keepdims=True)

    def build_op(i, carry):
        here = (iota((COLS, 4 * PTS), 0) + i * COLS).astype(F32)
        at = pl.ds(pl.multiple_of(i * COLS, COLS), COLS)
        for q in range(4):
            hit = jnp.where(here == cell_row[q : q + 1, :], 1.0, 0.0).astype(BF16)
            obs_op[at, 4 * K * q : 4 * K * (q + 1)] = lax.dot_general(
                hit, blocks[q], NT, preferred_element_type=F32
            ).astype(BF16)
        return carry

    lax.fori_loop(0, ROWS, build_op, 0)

    def wait_rs(k, carry):
        rs_copy(k).wait_recv()
        return carry

    lax.fori_loop(1, N_LON, wait_rs, 0)
    own = grad[pl.ds(pl.multiple_of(CHUNK * lon, 8), CHUNK), :]
    for k in range(1, N_LON):
        own += rs_buf[k]
    part[...] = own
    ex_buf[lat] = own

    def ex_copy(k):
        return pltpu.make_async_remote_copy(
            src_ref=part,
            dst_ref=ex_buf.at[lat],
            send_sem=ex_send.at[k],
            recv_sem=ex_recv.at[k],
            device_id=(lax.rem(lat + k, N_LAT), lon),
            device_id_type=MESH,
        )

    for k in range(1, N_LAT):
        ex_copy(k).start()

    model_obs = jnp.dot(
        jnp.concatenate([x_rows[1, i] for i in range(ROWS)], axis=1),
        obs_op[...],
        preferred_element_type=F32,
    ).T

    def p_row(which, place):
        pair = p_buf[which].astype(F32)
        return jnp.where(place == 0, pair[0:1, :], pair[1:2, :])

    pieces = []
    for t in range(TRACKS):
        value = v_buf[owners[t], places[t]].astype(F32)
        precision = p_row(owners[t], places[t])
        pieces.append((model_obs[K * t : K * (t + 1), :] - value) * precision)
    misfit_t = jnp.concatenate(pieces, axis=0).T.astype(BF16)

    def finish_rows(first, last):
        def one(i, carry):
            fields = []
            for a in range(3):
                row = i + 4 - 2 * a
                fields += [a_shift[0, row], a_rows[row], a_shift[1, row]]
            total = a_rows[i + 2].astype(F32) + jnp.dot(
                w_diag[...], jnp.concatenate(fields, axis=0), preferred_element_type=F32
            )
            at = pl.ds(pl.multiple_of(i * COLS, COLS), COLS)
            total += lax.dot_general(misfit_t, obs_op[at, :], NT, preferred_element_type=F32)
            for half in range(2):
                f_buf[half, pl.ds(i, CH, stride=ROWS), :] = total[
                    :, 128 * half : 128 * half + 128
                ]
            return carry

        lax.fori_loop(first, last, one, 0)

    for k in range(1, N_LAT):
        ex_copy(k).wait_recv()
    whole = ex_buf[0]
    for k in range(1, N_LAT):
        whole += ex_buf[k]
    mine = pl.ds(pl.multiple_of(CHUNK * lon, 8), CHUNK)
    gathered[mine, :] = whole

    def ag_copy(k):
        return pltpu.make_async_remote_copy(
            src_ref=gathered.at[mine, :],
            dst_ref=gathered.at[mine, :],
            send_sem=ag_send.at[k],
            recv_sem=ag_recv.at[k],
            device_id=(lat, lax.rem(lon + k, N_LON)),
            device_id_type=MESH,
        )

    def start_ag(k, carry):
        ag_copy(k).start()
        return carry

    lax.fori_loop(1, N_LON, start_ag, 0)
    finish_rows(0, ROWS)
    for half in range(2):
        out[:, :, 128 * half : 128 * half + 128] = (
            f_buf[half].reshape(CH, ROWS, 128).astype(BF16)
        )

    def wait_ag(k, carry):
        ag_copy(k).wait_recv()
        return carry

    lax.fori_loop(1, N_LON, wait_ag, 0)
    for g in range(groups):
        for a in range(3):
            if a < 2:
                at, shift = 96 * (g // 2), 64 * (g % 2) + GROUP * a
            else:
                at, shift = 384 + 96 * (g // 4), GROUP * (g % 4)
            value = turn(gathered[at : at + 96, :], -shift)[:, :GROUP]
            for b in range(3):
                grad_out[g, 3 * a + b] = value[GROUP * b : GROUP * (b + 1), :]

    for copy in halos:
        copy.wait_send()

    def wait_sends(k, carry):
        for copy in obs_copies(k):
            copy.wait_send()
        rs_copy(k).wait_send()
        ag_copy(k).wait_send()
        return carry

    lax.fori_loop(1, N_LON, wait_sends, 0)
    for k in range(1, N_LAT):
        ex_copy(k).wait_send()


def on_device(
    adjoint_in,
    layer_input,
    conv_weight,
    footprint,
    owner,
    obs_weight,
    obs_value,
    obs_precision,
    obs_count,
):
    anywhere = pl.BlockSpec(memory_space=pltpu.HBM)
    vmem = pl.BlockSpec(memory_space=pltpu.VMEM)
    return pl.pallas_call(
        kernel,
        out_shape=(
            jax.ShapeDtypeStruct((CH, ROWS, COLS), BF16),
            jax.ShapeDtypeStruct((CH // GROUP, 9, GROUP, GROUP), F32),
        ),
        in_specs=[anywhere] * 9,
        out_specs=(vmem, vmem),
        scratch_shapes=[
            pltpu.SMEM((TRACKS,), jnp.int32),
            pltpu.SMEM((2 * N_LON,), jnp.int32),
            pltpu.VMEM((TRACKS, PTS), jnp.int32),
            pltpu.VMEM((CH, ROWS, COLS), BF16),
            pltpu.VMEM((CH, ROWS, COLS), BF16),
            pltpu.VMEM((2, CELLS, 128), F32),
            pltpu.VMEM((ROWS + 4, CH, COLS), BF16),
            pltpu.VMEM((2, ROWS + 4, CH, COLS), BF16),
            pltpu.VMEM((3, ROWS, CH, COLS), BF16),
            pltpu.VMEM((2, CH, 128), BF16),
            pltpu.VMEM((2, 2 * ROWS, CH), BF16),
            pltpu.VMEM((6, 2 * ROWS, CH), BF16),
            pltpu.VMEM((128, CH), F32),
            pltpu.VMEM((2, CH, 128), F32),
            pltpu.VMEM((3, CH, 128), BF16),
            pltpu.VMEM((CH // GROUP, 9, GROUP, GROUP), BF16),
            pltpu.VMEM((CH, 9 * CH), BF16),
            pltpu.VMEM((CELLS, TRACKS * K), BF16),
            pltpu.VMEM((4, 4 * K, 4 * PTS), BF16),
            pltpu.VMEM((8, 4 * PTS), F32),
            pltpu.VMEM((2 * N_LON, K, PTS), BF16),
            pltpu.VMEM((2 * N_LON, CH), BF16),
            pltpu.VMEM((N_LON, K, 2 * PTS), BF16),
            pltpu.VMEM((N_LON, 2, CH), BF16),
            pltpu.VMEM((N_LON, K, 2 * PTS), BF16),
            pltpu.VMEM((N_LON, 2, K, CH), BF16),
            pltpu.VMEM((N_LON, 2, CH), BF16),
            pltpu.VMEM((640, 128), F32),
            pltpu.VMEM((CH // GROUP, 96, 128), F32),
            pltpu.VMEM((N_LON, CHUNK, 128), F32),
            pltpu.VMEM((CHUNK, 128), F32),
            pltpu.VMEM((N_LAT, CHUNK, 128), F32),
            pltpu.VMEM((640, 128), F32),
            pltpu.SemaphoreType.DMA((9,)),
            pltpu.SemaphoreType.DMA((10,)),
            pltpu.SemaphoreType.DMA((10,)),
            pltpu.SemaphoreType.DMA((3, N_LON)),
            pltpu.SemaphoreType.DMA((3, N_LON)),
            pltpu.SemaphoreType.DMA((N_LON,)),
            pltpu.SemaphoreType.DMA((N_LON,)),
            pltpu.SemaphoreType.DMA((N_LAT,)),
            pltpu.SemaphoreType.DMA((N_LAT,)),
            pltpu.SemaphoreType.DMA((N_LON,)),
            pltpu.SemaphoreType.DMA((N_LON,)),
        ],
        compiler_params=pltpu.CompilerParams(
            collective_id=0, has_side_effects=True, vmem_limit_bytes=44 * 1024 * 1024
        ),
    )(
        *(
            pltpu.with_memory_space_constraint(value, pltpu.HBM)
            for value in (
                owner.reshape(TRACKS),
                obs_count,
                footprint,
                adjoint_in,
                layer_input,
                conv_weight,
                obs_weight,
                obs_value.reshape(N_LON, 2, K, CH),
                obs_precision,
            )
        ),
    )


def solution(mesh):
    in_specs = (
        P(None, "lat", "lon"),
        P(None, "lat", "lon"),
        P(),
        P(("lat", "lon"), None),
        P(("lat", "lon"), None),
        P(("lat", "lon"), None, None),
        P(("lat", "lon"), None, None),
        P(("lat", "lon"), None),
        P(("lat", "lon")),
    )
    out_specs = (P(None, "lat", "lon"), P())
    return jax.shard_map(
        on_device, mesh=mesh, in_specs=in_specs, out_specs=out_specs, check_vma=False
    )
```

time: 50.5 us -> 39.8 us (0.79)
  local copies, waits for them, and re-layouts: 7.05 us -> 1.99 us
  Pallas kernels: 40.7 us -> 37 us
  other arithmetic: 1.55 us -> 0 us
    pallas_call x1, Pallas kernels: 40.7 us -> 37 us  [on_device(): pl.pallas_call(kernel, out_shape=(jax.ShapeDtypeStruct((CH, ROWS, COLS),...]
    unnamed x10 -> x2, local copies, waits for them, and re-layouts: 4.38 us -> 1.99 us
    transpose x1 -> x0, local copies, waits for them, and re-layouts: 1.17 us -> none  [on_device(): weight_grad = grad.reshape(9, 2, GROUP, 4, GROUP).transpose(1, 3, 0, 2, 4)]
    another operation x3 -> x0, local copies, waits for them, and re-layouts: 0.92 us -> none  [on_device(): jnp.stack([obs_precision, counts], axis=1).reshape(N_LON, 2, 2, CH)]
    convert_element_type x1 -> x0, other arithmetic: 0.75 us -> none  [on_device(): counts = jnp.broadcast_to(obs_count[:, None], (2 * N_LON, CH)).astype(BF16)]
    add x1 -> x0, other arithmetic: 0.72 us -> none  [on_device(): (footprint // full_width - lat_start) * COLS]
    reshape x2 -> x0, local copies, waits for them, and re-layouts: 0.58 us -> none  [the longest x1 0.5 us: on_device(): weight_grad = grad.reshape(9, 2, GROUP, 4, GROUP).transpose(1, 3, 0, 2, 4)]
where the time goes in v2:
time: 39.8 us; the launch traced here: 39.6 us
  Pallas kernels  37 us (93%)
  local copies, waits for them, and re-layouts  1.99 us (5%)
  between operations  0.64 us (2%)
    pallas_call x1, Pallas kernels, on_device(): pl.pallas_call(kernel, out_shape=(jax.ShapeDtypeStruct((CH, ROWS, COLS),...  37 us
    unnamed x2, local copies, waits for them, and re-layouts  1.99 us

profile of v2, /device:TPU:1, one launch (start us, length us, event | category | flops | bytes accessed | tf_op | source)
XLA Modules:
  0.0 39.6 jit_solution(8023163863329664684)
XLA Ops:
  0.6 37.0 %shard_map.104 = (bf16[256,8,256]{2,1,0:T(8,128)(2,1)S(1)}, f32[8,9,32,32]{3,2,1,0:T(8,128)S(1)}) custom-call(s32[16]{0:T(128)} %bitcast.3, s32[32]{0:T(128)} %counts_in.1, s32[16,64]{1,0:T(8,128)} %fp_in.1, bf16[256,8,256]{2,1,0:T(8,128)(2,1)} %adj_in.1, bf16[256,8,256]{2,1,0:T(8,128)(2,1)} %x_in.1, bf16[8,9,32,32]{3,2,1,0:T(8,128)(2,1)} %conv_w.1, ...), custom_call_target="tpu_custom_call" | custom-call | tf_op jit(solution)/shard_map/pallas_call | solution.py:549
  37.7 1.0 %copy.13 = bf16[256,8,256]{2,1,0:T(8,128)(2,1)} copy(bf16[256,8,256]{2,1,0:T(8,128)(2,1)S(1)} %get-tuple-element.4) | data formatting | bytes 2097152
  38.6 1.0 %copy.14 = f32[8,9,32,32]{3,2,1,0:T(8,128)} copy(f32[8,9,32,32]{3,2,1,0:T(8,128)S(1)} %get-tuple-element.5) | data formatting | bytes 589824

commit v3 on v2

--- a/solution.py
+++ b/solution.py
@@ -18,11 +18,16 @@
 TRACKS = 16
 K = 32
 PTS = 64
-CHUNK = 40
+CHUNK = 5
 CB = 64
 F32 = jnp.float32
 BF16 = jnp.bfloat16
 NT = (((1,), (1,)), ((), ()))
+STEPS = sorted(
+    ((a, b) for a in range(4) for b in range(4) if a or b),
+    key=lambda step: -min(step[0], 4 - step[0]) - min(step[1], 4 - step[1]),
+)
+PACK = 96
 
 
 def iota(shape, dim):
@@ -62,16 +67,15 @@
     a_edge,
     w_in,
     w_diag,
+    total,
     obs_op,
     blocks,
     cell_row,
     w_nat,
     p_nat,
-    w_own,
-    p_own,
-    w_buf,
-    v_buf,
-    p_buf,
+    packed,
+    early,
+    late,
     grad,
     g_acc,
     rs_buf,
@@ -96,6 +100,8 @@
     south = lax.rem(lat + 1, N_LAT)
     west = lax.rem(lon + N_LON - 1, N_LON)
     east = lax.rem(lon + 1, N_LON)
+    outer, inner = lon // 4, lax.rem(lon, 4)
+    peers = [4 * lax.rem(outer + a, 4) + lax.rem(inner + b, 4) for a, b in STEPS]
 
     local = [
         pltpu.make_async_copy(src, dst, local_sem.at[index])
@@ -106,7 +112,8 @@
                 (obs_w, w_nat),
                 (obs_p, p_nat),
                 (conv_w, w_in),
-                (obs_v.at[lon], v_buf.at[lon]),
+                (obs_v.at[:, 0], packed.at[:, pl.ds(0, K), :]),
+                (obs_v.at[:, 1], packed.at[:, pl.ds(2 * K, K), :]),
                 (owner_in, owner),
                 (counts_in, counts),
                 (fp_in, fp),
@@ -125,8 +132,8 @@
         greet(to_lat, to_lon)
     for k in range(1, N_LAT):
         greet(lax.rem(lat + k, N_LAT), lon)
-    for k in range(1, N_LON):
-        greet(lat, lax.rem(lon + k, N_LON))
+    for peer in peers:
+        greet(lat, peer)
 
     lane = iota((CB, 128), 1)
 
@@ -161,16 +168,21 @@
 
     local[2].wait()
     local[3].wait()
-    local[7].wait()
+    local[8].wait()
     obs_row = iota((K, PTS), 0)
     for s in range(2 * N_LON):
-        w_own[s // 2, :, PTS * (s % 2) : PTS * (s % 2 + 1)] = jnp.where(
+        packed[s // 2, K : 2 * K, PTS * (s % 2) : PTS * (s % 2 + 1)] = jnp.where(
             obs_row < counts[s], w_nat[s].astype(F32), 0.0
         ).astype(BF16)
-    for s in range(N_LON):
-        p_own[s] = p_nat[2 * s : 2 * s + 2, :]
-    w_buf[lon] = w_own[lon]
-    p_buf[lon] = p_own[lon]
+        for half in range(2):
+            at = K + 2 * (s % 2) + half
+            packed[s // 2, at : at + 1, 128:] = p_nat[
+                s : s + 1, 128 * half : 128 * half + 128
+            ]
+    local[5].wait()
+    local[6].wait()
+    early[lon] = packed[lon, : 2 * K]
+    late[lon] = packed[lon, 2 * K :]
 
     local[1].wait()
 
@@ -220,6 +232,23 @@
         stacked = jnp.concatenate([w_in[g, tap] for g in range(groups)], axis=0)
         tiled = jnp.dot(stacked, spread, preferred_element_type=F32)
         w_diag[:, CH * tap : CH * (tap + 1)] = jnp.where(same_group, tiled, 0.0).astype(BF16)
+
+    def weigh(taps, fields):
+        weights = [w_diag[:, CH * tap : CH * (tap + 1)] for tap in taps]
+        return jnp.dot(
+            jnp.concatenate(weights, axis=1),
+            jnp.concatenate(fields, axis=0),
+            preferred_element_type=F32,
+        )
+
+    def rows_of_taps(i):
+        return [(a, i + 4 - 2 * a, 2 <= i + 4 - 2 * a < ROWS + 2) for a in range(3)]
+
+    for i in range(ROWS):
+        here = [(a, row) for a, row, own_row in rows_of_taps(i) if own_row]
+        total[i] = a_rows[i + 2].astype(F32) + weigh(
+            [3 * a + 1 for a, _ in here], [a_rows[row] for _, row in here]
+        )
 
     pl.semaphore_wait(barrier, 4 + N_LAT - 1 + N_LON - 1)
 
@@ -256,28 +285,19 @@
     for copy in halos:
         copy.start()
 
-    def obs_copies(k):
-        peer = lax.rem(lon + k, N_LON)
-        return [
-            pltpu.make_async_remote_copy(
-                src_ref=src.at[peer],
-                dst_ref=dst.at[lon],
-                send_sem=obs_send.at[index, k],
-                recv_sem=obs_recv.at[index, k],
-                device_id=(lat, peer),
-                device_id_type=MESH,
-            )
-            for index, (src, dst) in enumerate(
-                ((w_own, w_buf), (obs_v, v_buf), (p_own, p_buf))
-            )
-        ]
-
-    def start_obs(k, carry):
-        for copy in obs_copies(k):
-            copy.start()
-        return carry
-
-    lax.fori_loop(1, N_LON, start_obs, 0)
+    def obs_copy(k, which):
+        at = (pl.ds(0, 2 * K), pl.ds(2 * K, K))[which]
+        return pltpu.make_async_remote_copy(
+            src_ref=packed.at[peers[k], at],
+            dst_ref=(early, late)[which].at[lon],
+            send_sem=obs_send.at[which, k],
+            recv_sem=obs_recv.at[which, k],
+            device_id=(lat, peers[k]),
+            device_id_type=MESH,
+        )
+
+    for k in range(N_LON - 1):
+        obs_copy(k, 0).start()
 
     for copy in halos[:6]:
         copy.wait_recv()
@@ -300,6 +320,10 @@
     nothing = jnp.zeros((GROUP, 128), BF16)
     tile_lane = iota((3 * GROUP, 128), 1)
     done = []
+
+    def put_grad(at, value):
+        grad[at : at + 12] = value.reshape(12, 8, 128).astype(BF16)
+
     for g in range(groups):
         if g % 4 == 0:
             half = pl.ds(CH // 2 * (g // 4), CH // 2)
@@ -318,36 +342,32 @@
         moved, meets = meeting(g, (0, 1, ROWS - 2, ROWS - 1))
         moved.append(jnp.concatenate([x_edge[0, at, :], nothing, x_edge[1, at, :]], axis=0))
         meets.append(jnp.concatenate([a_edge[a, at, :] for a in (0, 1, 2, 2)], axis=0))
-        total = (pair_up(moved, meets) + g_acc[g]) * scale
-        done.append(total)
+        value = (pair_up(moved, meets) + g_acc[g]) * scale
+        done.append(value)
         if g % 2 == 1:
-            at = 96 * (g // 2)
-            grad[at : at + 96, :] = jnp.where(tile_lane < 64, done[g - 1], turn(total, 64))
+            put_grad(12 * (g // 2), jnp.where(tile_lane < 64, done[g - 1], turn(value, 64)))
         if g % 4 == 3:
             value = turn(done[g - 3], -64)
             for m in range(1, 4):
                 shifted = turn(done[g - 3 + m], 32 * m - 64)
                 value = jnp.where(tile_lane // GROUP == m, shifted, value)
-            at = 384 + 96 * (g // 4)
-            grad[at : at + 96, :] = value
-    grad[576:640, :] = jnp.zeros((64, 128), F32)
+            put_grad(48 + 12 * (g // 4), value)
+    grad[72:] = jnp.zeros((8, 8, 128), BF16)
 
     def rs_copy(k):
-        peer = lax.rem(lon + k, N_LON)
         return pltpu.make_async_remote_copy(
-            src_ref=grad.at[pl.ds(pl.multiple_of(CHUNK * peer, 8), CHUNK), :],
+            src_ref=grad.at[pl.ds(CHUNK * peers[k], CHUNK)],
             dst_ref=rs_buf.at[k],
             send_sem=rs_send.at[k],
             recv_sem=rs_recv.at[k],
-            device_id=(lat, peer),
+            device_id=(lat, peers[k]),
             device_id_type=MESH,
         )
 
-    def start_rs(k, carry):
+    for k in range(N_LON - 1):
         rs_copy(k).start()
-        return carry
-
-    lax.fori_loop(1, N_LON, start_rs, 0)
+    for k in range(N_LON - 1):
+        obs_copy(k, 1).start()
 
     for row in range(ROWS + 4):
         for c in range(0, CH, CB):
@@ -363,15 +383,10 @@
             a_shift[1, row, at, :128] = jnp.where(lane < 2, west_cols, low_back).astype(BF16)
             a_shift[1, row, at, 128:] = jnp.where(lane < 2, low_back, high_back).astype(BF16)
 
-    for copy in (local[5], local[6], local[8]):
+    for copy in (local[7], local[9]):
         copy.wait()
-
-    def wait_obs(k, carry):
-        for copy in obs_copies(k):
-            copy.wait_recv()
-        return carry
-
-    lax.fori_loop(1, N_LON, wait_obs, 0)
+    for k in range(N_LON - 1):
+        obs_copy(k, 0).wait_recv()
     owners = [owner[t] for t in range(TRACKS)]
     places = [
         jnp.minimum(
@@ -395,7 +410,7 @@
     for q in range(4):
         tracks = range(4 * q, 4 * q + 4)
         stacked = jnp.concatenate(
-            [jnp.where(slot_lane == places[t], w_buf[owners[t]].astype(F32), 0.0) for t in tracks],
+            [jnp.where(slot_lane == places[t], early[owners[t], K : 2 * K, :128].astype(F32), 0.0) for t in tracks],
             axis=0,
         )
         tiled = jnp.dot(stacked.astype(BF16), widen_pair, preferred_element_type=F32)
@@ -414,14 +429,10 @@
 
     lax.fori_loop(0, ROWS, build_op, 0)
 
-    def wait_rs(k, carry):
+    own = grad[pl.ds(CHUNK * lon, CHUNK)].astype(F32)
+    for k in range(N_LON - 1):
         rs_copy(k).wait_recv()
-        return carry
-
-    lax.fori_loop(1, N_LON, wait_rs, 0)
-    own = grad[pl.ds(pl.multiple_of(CHUNK * lon, 8), CHUNK), :]
-    for k in range(1, N_LON):
-        own += rs_buf[k]
+        own += rs_buf[k].astype(F32)
     part[...] = own
     ex_buf[lat] = own
 
@@ -445,92 +456,102 @@
     ).T
 
     def p_row(which, place):
-        pair = p_buf[which].astype(F32)
-        return jnp.where(place == 0, pair[0:1, :], pair[1:2, :])
+        rows = early[which, K : K + 4, 128:].astype(F32)
+        first = jnp.concatenate([rows[0:1, :], rows[1:2, :]], axis=1)
+        second = jnp.concatenate([rows[2:3, :], rows[3:4, :]], axis=1)
+        return jnp.where(place == 0, first, second)
 
     pieces = []
+    for k in range(N_LON - 1):
+        obs_copy(k, 1).wait_recv()
     for t in range(TRACKS):
-        value = v_buf[owners[t], places[t]].astype(F32)
+        value = jnp.where(
+            places[t] == 0,
+            early[owners[t], :K, :].astype(F32),
+            late[owners[t]].astype(F32),
+        )
         precision = p_row(owners[t], places[t])
         pieces.append((model_obs[K * t : K * (t + 1), :] - value) * precision)
     misfit_t = jnp.concatenate(pieces, axis=0).T.astype(BF16)
 
-    def finish_rows(first, last):
-        def one(i, carry):
-            fields = []
-            for a in range(3):
-                row = i + 4 - 2 * a
-                fields += [a_shift[0, row], a_rows[row], a_shift[1, row]]
-            total = a_rows[i + 2].astype(F32) + jnp.dot(
-                w_diag[...], jnp.concatenate(fields, axis=0), preferred_element_type=F32
+    def finish_row(i):
+        taps, fields = [], []
+        for a, row, own_row in rows_of_taps(i):
+            taps += [3 * a, 3 * a + 2]
+            fields += [a_shift[0, row], a_shift[1, row]]
+            if not own_row:
+                taps.append(3 * a + 1)
+                fields.append(a_rows[row])
+        done_row = (
+            total[i]
+            + weigh(taps, fields)
+            + lax.dot_general(
+                misfit_t,
+                obs_op[COLS * i : COLS * (i + 1), :],
+                NT,
+                preferred_element_type=F32,
             )
-            at = pl.ds(pl.multiple_of(i * COLS, COLS), COLS)
-            total += lax.dot_general(misfit_t, obs_op[at, :], NT, preferred_element_type=F32)
-            for half in range(2):
-                f_buf[half, pl.ds(i, CH, stride=ROWS), :] = total[
-                    :, 128 * half : 128 * half + 128
-                ]
-            return carry
-
-        lax.fori_loop(first, last, one, 0)
+        )
+        for half in range(2):
+            f_buf[half, pl.ds(i, CH, stride=ROWS), :] = done_row[:, 128 * half : 128 * half + 128]
 
     for k in range(1, N_LAT):
         ex_copy(k).wait_recv()
     whole = ex_buf[0]
     for k in range(1, N_LAT):
         whole += ex_buf[k]
-    mine = pl.ds(pl.multiple_of(CHUNK * lon, 8), CHUNK)
-    gathered[mine, :] = whole
+    mine = pl.ds(CHUNK * lon, CHUNK)
+    gathered[mine] = whole.astype(BF16)
 
     def ag_copy(k):
         return pltpu.make_async_remote_copy(
-            src_ref=gathered.at[mine, :],
-            dst_ref=gathered.at[mine, :],
+            src_ref=gathered.at[mine],
+            dst_ref=gathered.at[mine],
             send_sem=ag_send.at[k],
             recv_sem=ag_recv.at[k],
-            device_id=(lat, lax.rem(lon + k, N_LON)),
+            device_id=(lat, peers[k]),
             device_id_type=MESH,
         )
 
-    def start_ag(k, carry):
+    for k in range(N_LON - 1):
         ag_copy(k).start()
-        return carry
-
-    lax.fori_loop(1, N_LON, start_ag, 0)
-    finish_rows(0, ROWS)
+    for i in range(ROWS):
+        finish_row(i)
     for half in range(2):
         out[:, :, 128 * half : 128 * half + 128] = (
             f_buf[half].reshape(CH, ROWS, 128).astype(BF16)
         )
 
-    def wait_ag(k, carry):
+    for copy in halos:
+        copy.wait_send()
+    for k in range(1, N_LAT):
+        ex_copy(k).wait_send()
+    for k in range(N_LON - 1):
+        obs_copy(k, 0).wait_send()
+        obs_copy(k, 1).wait_send()
+        rs_copy(k).wait_send()
+        ag_copy(k).wait_send()
+    for k in range(N_LON - 1):
         ag_copy(k).wait_recv()
-        return carry
-
-    lax.fori_loop(1, N_LON, wait_ag, 0)
-    for g in range(groups):
+    grad_out[...] = gathered[...]
+
+
+def unpack(field, grad, out, grad_out, blocks, sem):
+    copy = pltpu.make_async_copy(field, out, sem.at[0])
+    copy.start()
+    for g in range(CH // GROUP):
         for a in range(3):
             if a < 2:
-                at, shift = 96 * (g // 2), 64 * (g % 2) + GROUP * a
+                at, shift = 12 * (g // 2), 64 * (g % 2) + GROUP * a
             else:
-                at, shift = 384 + 96 * (g // 4), GROUP * (g % 4)
-            value = turn(gathered[at : at + 96, :], -shift)[:, :GROUP]
+                at, shift = 48 + 12 * (g // 4), GROUP * (g % 4)
+            value = turn(grad[at : at + 12].astype(F32).reshape(96, 128), -shift)[:, :GROUP]
             for b in range(3):
-                grad_out[g, 3 * a + b] = value[GROUP * b : GROUP * (b + 1), :]
-
-    for copy in halos:
-        copy.wait_send()
-
-    def wait_sends(k, carry):
-        for copy in obs_copies(k):
-            copy.wait_send()
-        rs_copy(k).wait_send()
-        ag_copy(k).wait_send()
-        return carry
-
-    lax.fori_loop(1, N_LON, wait_sends, 0)
-    for k in range(1, N_LAT):
-        ex_copy(k).wait_send()
+                blocks[g, 3 * a + b] = value[GROUP * b : GROUP * (b + 1), :]
+    copy_grad = pltpu.make_async_copy(blocks, grad_out, sem.at[1])
+    copy_grad.start()
+    copy.wait()
+    copy_grad.wait()
 
 
 def on_device(
@@ -546,11 +567,11 @@
 ):
     anywhere = pl.BlockSpec(memory_space=pltpu.HBM)
     vmem = pl.BlockSpec(memory_space=pltpu.VMEM)
-    return pl.pallas_call(
+    field, grad = pl.pallas_call(
         kernel,
         out_shape=(
             jax.ShapeDtypeStruct((CH, ROWS, COLS), BF16),
-            jax.ShapeDtypeStruct((CH // GROUP, 9, GROUP, GROUP), F32),
+            jax.ShapeDtypeStruct((N_LON * CHUNK, 8, 128), BF16),
         ),
         in_specs=[anywhere] * 9,
         out_specs=(vmem, vmem),
@@ -572,27 +593,26 @@
             pltpu.VMEM((3, CH, 128), BF16),
             pltpu.VMEM((CH // GROUP, 9, GROUP, GROUP), BF16),
             pltpu.VMEM((CH, 9 * CH), BF16),
+            pltpu.VMEM((ROWS, CH, COLS), F32),
             pltpu.VMEM((CELLS, TRACKS * K), BF16),
             pltpu.VMEM((4, 4 * K, 4 * PTS), BF16),
             pltpu.VMEM((8, 4 * PTS), F32),
             pltpu.VMEM((2 * N_LON, K, PTS), BF16),
             pltpu.VMEM((2 * N_LON, CH), BF16),
-            pltpu.VMEM((N_LON, K, 2 * PTS), BF16),
-            pltpu.VMEM((N_LON, 2, CH), BF16),
-            pltpu.VMEM((N_LON, K, 2 * PTS), BF16),
-            pltpu.VMEM((N_LON, 2, K, CH), BF16),
-            pltpu.VMEM((N_LON, 2, CH), BF16),
-            pltpu.VMEM((640, 128), F32),
+            pltpu.VMEM((N_LON, PACK, CH), BF16),
+            pltpu.VMEM((N_LON, 2 * K, CH), BF16),
+            pltpu.VMEM((N_LON, K, CH), BF16),
+            pltpu.VMEM((N_LON * CHUNK, 8, 128), BF16),
             pltpu.VMEM((CH // GROUP, 96, 128), F32),
-            pltpu.VMEM((N_LON, CHUNK, 128), F32),
-            pltpu.VMEM((CHUNK, 128), F32),
-            pltpu.VMEM((N_LAT, CHUNK, 128), F32),
-            pltpu.VMEM((640, 128), F32),
-            pltpu.SemaphoreType.DMA((9,)),
+            pltpu.VMEM((N_LON, CHUNK, 8, 128), BF16),
+            pltpu.VMEM((CHUNK, 8, 128), F32),
+            pltpu.VMEM((N_LAT, CHUNK, 8, 128), F32),
+            pltpu.VMEM((N_LON * CHUNK, 8, 128), BF16),
             pltpu.SemaphoreType.DMA((10,)),
             pltpu.SemaphoreType.DMA((10,)),
-            pltpu.SemaphoreType.DMA((3, N_LON)),
-            pltpu.SemaphoreType.DMA((3, N_LON)),
+            pltpu.SemaphoreType.DMA((10,)),
+            pltpu.SemaphoreType.DMA((2, N_LON)),
+            pltpu.SemaphoreType.DMA((2, N_LON)),
             pltpu.SemaphoreType.DMA((N_LON,)),
             pltpu.SemaphoreType.DMA((N_LON,)),
             pltpu.SemaphoreType.DMA((N_LAT,)),
@@ -619,6 +639,20 @@
             )
         ),
     )
+    return pl.pallas_call(
+        unpack,
+        out_shape=(
+            jax.ShapeDtypeStruct((CH, ROWS, COLS), BF16),
+            jax.ShapeDtypeStruct((CH // GROUP, 9, GROUP, GROUP), F32),
+        ),
+        in_specs=[vmem, vmem],
+        out_specs=(pl.BlockSpec(memory_space=pl.ANY), pl.BlockSpec(memory_space=pl.ANY)),
+        scratch_shapes=[
+            pltpu.VMEM((CH // GROUP, 9, GROUP, GROUP), F32),
+            pltpu.SemaphoreType.DMA((2,)),
+        ],
+        compiler_params=pltpu.CompilerParams(vmem_limit_bytes=8 * 1024 * 1024),
+    )(field, grad)
 
 
 def solution(mesh):

time: 39.8 us -> 34.5 us (0.87)
  Pallas kernels: 37 us -> 33.8 us
  local copies, waits for them, and re-layouts: 1.99 us -> 0 us
    pallas_call x1, Pallas kernels: 37 us -> 32.4 us  [on_device(): pl.pallas_call(kernel, out_shape=(jax.ShapeDtypeStruct((CH, ROWS, COLS),...]
    unnamed x2 -> x0, local copies, waits for them, and re-layouts: 1.99 us -> none
    pallas_call x0 -> x1, Pallas kernels: none -> 1.38 us  [on_device(): pl.pallas_call(unpack, out_shape=(jax.ShapeDtypeStruct((CH, ROWS, COLS),...]
where the time goes in v3:
time: 34.5 us; the launch traced here: 34.4 us
  Pallas kernels  33.8 us (98%)
  between operations  0.64 us (2%)
    pallas_call x1, Pallas kernels, on_device(): pl.pallas_call(kernel, out_shape=(jax.ShapeDtypeStruct((CH, ROWS, COLS),...  32.4 us
    pallas_call x1, Pallas kernels, on_device(): pl.pallas_call(unpack, out_shape=(jax.ShapeDtypeStruct((CH, ROWS, COLS),...  1.38 us

profile of v3, /device:TPU:1, one launch (start us, length us, event | category | flops | bytes accessed | tf_op | source)
XLA Modules:
  0.0 34.4 jit_solution(14951098724107570612)
XLA Ops:
  0.6 32.4 %shard_map.104 = (bf16[256,8,256]{2,1,0:T(8,128)(2,1)S(1)}, bf16[80,8,128]{2,1,0:T(8,128)(2,1)S(1)}) custom-call(s32[16]{0:T(128)} %bitcast.3, s32[32]{0:T(128)} %counts_in.1, s32[16,64]{1,0:T(8,128)} %fp_in.1, bf16[256,8,256]{2,1,0:T(8,128)(2,1)} %adj_in.1, bf16[256,8,256]{2,1,0:T(8,128)(2,1)} %x_in.1, bf16[8,9,32,32]{3,2,1,0:T(8,128)(2,1)} %conv_w.1, ...), custom_call_target="tpu_custom_call" | custom-call | tf_op jit(solution)/shard_map/pallas_call | solution.py:570
  33.0 1.4 %shard_map.105 = (bf16[256,8,256]{2,1,0:T(8,128)(2,1)}, f32[8,9,32,32]{3,2,1,0:T(8,128)}) custom-call(bf16[256,8,256]{2,1,0:T(8,128)(2,1)S(1)} %get-tuple-element.4.field, bf16[80,8,128]{2,1,0:T(8,128)(2,1)S(1)} %get-tuple-element.5.grad), custom_call_target="tpu_custom_call" | custom-call | tf_op jit(solution)/shard_map/pallas_call | solution.py:642

commit v4 on v3

--- a/solution.py
+++ b/solution.py
@@ -433,8 +433,8 @@
     for k in range(N_LON - 1):
         rs_copy(k).wait_recv()
         own += rs_buf[k].astype(F32)
-    part[...] = own
-    ex_buf[lat] = own
+    part[...] = own.astype(BF16)
+    ex_buf[lat] = own.astype(BF16)
 
     def ex_copy(k):
         return pltpu.make_async_remote_copy(
@@ -446,7 +446,7 @@
             device_id_type=MESH,
         )
 
-    for k in range(1, N_LAT):
+    for k in (4, 3, 5, 2, 6, 1, 7):
         ex_copy(k).start()
 
     model_obs = jnp.dot(
@@ -497,9 +497,9 @@
 
     for k in range(1, N_LAT):
         ex_copy(k).wait_recv()
-    whole = ex_buf[0]
+    whole = ex_buf[0].astype(F32)
     for k in range(1, N_LAT):
-        whole += ex_buf[k]
+        whole += ex_buf[k].astype(F32)
     mine = pl.ds(CHUNK * lon, CHUNK)
     gathered[mine] = whole.astype(BF16)
 
@@ -605,8 +605,8 @@
             pltpu.VMEM((N_LON * CHUNK, 8, 128), BF16),
             pltpu.VMEM((CH // GROUP, 96, 128), F32),
             pltpu.VMEM((N_LON, CHUNK, 8, 128), BF16),
-            pltpu.VMEM((CHUNK, 8, 128), F32),
-            pltpu.VMEM((N_LAT, CHUNK, 8, 128), F32),
+            pltpu.VMEM((CHUNK, 8, 128), BF16),
+            pltpu.VMEM((N_LAT, CHUNK, 8, 128), BF16),
             pltpu.VMEM((N_LON * CHUNK, 8, 128), BF16),
             pltpu.SemaphoreType.DMA((10,)),
             pltpu.SemaphoreType.DMA((10,)),

time: 34.5 us -> 34 us (0.986)
  Pallas kernels: 33.8 us -> 33.2 us
    pallas_call x1, Pallas kernels: 32.4 us -> 31.8 us  [on_device(): pl.pallas_call(kernel, out_shape=(jax.ShapeDtypeStruct((CH, ROWS, COLS),...]
where the time goes in v4:
time: 34 us; the launch traced here: 33.9 us
  Pallas kernels  33.2 us (98%)
  between operations  0.64 us (2%)
    pallas_call x1, Pallas kernels, on_device(): pl.pallas_call(kernel, out_shape=(jax.ShapeDtypeStruct((CH, ROWS, COLS),...  31.8 us
    pallas_call x1, Pallas kernels, on_device(): pl.pallas_call(unpack, out_shape=(jax.ShapeDtypeStruct((CH, ROWS, COLS),...  1.38 us

profile of v4, /device:TPU:1, one launch (start us, length us, event | category | flops | bytes accessed | tf_op | source)
XLA Modules:
  0.0 33.9 jit_solution(11486036698977754508)
XLA Ops:
  0.6 31.8 %shard_map.104 = (bf16[256,8,256]{2,1,0:T(8,128)(2,1)S(1)}, bf16[80,8,128]{2,1,0:T(8,128)(2,1)S(1)}) custom-call(s32[16]{0:T(128)} %bitcast.3, s32[32]{0:T(128)} %counts_in.1, s32[16,64]{1,0:T(8,128)} %fp_in.1, bf16[256,8,256]{2,1,0:T(8,128)(2,1)} %adj_in.1, bf16[256,8,256]{2,1,0:T(8,128)(2,1)} %x_in.1, bf16[8,9,32,32]{3,2,1,0:T(8,128)(2,1)} %conv_w.1, ...), custom_call_target="tpu_custom_call" | custom-call | tf_op jit(solution)/shard_map/pallas_call | solution.py:570
  32.5 1.4 %shard_map.105 = (bf16[256,8,256]{2,1,0:T(8,128)(2,1)}, f32[8,9,32,32]{3,2,1,0:T(8,128)}) custom-call(bf16[256,8,256]{2,1,0:T(8,128)(2,1)S(1)} %get-tuple-element.4.field, bf16[80,8,128]{2,1,0:T(8,128)(2,1)S(1)} %get-tuple-element.5.grad), custom_call_target="tpu_custom_call" | custom-call | tf_op jit(solution)/shard_map/pallas_call | solution.py:642

commit v5 on v3

--- a/solution.py
+++ b/solution.py
@@ -446,7 +446,7 @@
             device_id_type=MESH,
         )
 
-    for k in range(1, N_LAT):
+    for k in (4, 3, 5, 2, 6, 1, 7):
         ex_copy(k).start()
 
     model_obs = jnp.dot(
@@ -454,6 +454,27 @@
         obs_op[...],
         preferred_element_type=F32,
     ).T
+
+    for k in range(1, N_LAT):
+        ex_copy(k).wait_recv()
+    whole = ex_buf[0]
+    for k in range(1, N_LAT):
+        whole += ex_buf[k]
+    mine = pl.ds(CHUNK * lon, CHUNK)
+    gathered[mine] = whole.astype(BF16)
+
+    def ag_copy(k):
+        return pltpu.make_async_remote_copy(
+            src_ref=gathered.at[mine],
+            dst_ref=gathered.at[mine],
+            send_sem=ag_send.at[k],
+            recv_sem=ag_recv.at[k],
+            device_id=(lat, peers[k]),
+            device_id_type=MESH,
+        )
+
+    for k in range(N_LON - 1):
+        ag_copy(k).start()
 
     def p_row(which, place):
         rows = early[which, K : K + 4, 128:].astype(F32)
@@ -495,26 +516,6 @@
         for half in range(2):
             f_buf[half, pl.ds(i, CH, stride=ROWS), :] = done_row[:, 128 * half : 128 * half + 128]
 
-    for k in range(1, N_LAT):
-        ex_copy(k).wait_recv()
-    whole = ex_buf[0]
-    for k in range(1, N_LAT):
-        whole += ex_buf[k]
-    mine = pl.ds(CHUNK * lon, CHUNK)
-    gathered[mine] = whole.astype(BF16)
-
-    def ag_copy(k):
-        return pltpu.make_async_remote_copy(
-            src_ref=gathered.at[mine],
-            dst_ref=gathered.at[mine],
-            send_sem=ag_send.at[k],
-            recv_sem=ag_recv.at[k],
-            device_id=(lat, peers[k]),
-            device_id_type=MESH,
-        )
-
-    for k in range(N_LON - 1):
-        ag_copy(k).start()
     for i in range(ROWS):
         finish_row(i)
     for half in range(2):

time: 34.5 us -> 34.1 us (0.988)
  Pallas kernels: 33.8 us -> 33.3 us
    pallas_call x1, Pallas kernels: 32.4 us -> 31.9 us  [on_device(): pl.pallas_call(kernel, out_shape=(jax.ShapeDtypeStruct((CH, ROWS, COLS),...]
where the time goes in v5:
time: 34.1 us; the launch traced here: 34 us
  Pallas kernels  33.3 us (98%)
  between operations  0.64 us (2%)
    pallas_call x1, Pallas kernels, on_device(): pl.pallas_call(kernel, out_shape=(jax.ShapeDtypeStruct((CH, ROWS, COLS),...  31.9 us
    pallas_call x1, Pallas kernels, on_device(): pl.pallas_call(unpack, out_shape=(jax.ShapeDtypeStruct((CH, ROWS, COLS),...  1.38 us

profile of v5, /device:TPU:1, one launch (start us, length us, event | category | flops | bytes accessed | tf_op | source)
XLA Modules:
  0.0 34.0 jit_solution(10460624885942697432)
XLA Ops:
  0.6 31.9 %shard_map.104 = (bf16[256,8,256]{2,1,0:T(8,128)(2,1)S(1)}, bf16[80,8,128]{2,1,0:T(8,128)(2,1)S(1)}) custom-call(s32[16]{0:T(128)} %bitcast.3, s32[32]{0:T(128)} %counts_in.1, s32[16,64]{1,0:T(8,128)} %fp_in.1, bf16[256,8,256]{2,1,0:T(8,128)(2,1)} %adj_in.1, bf16[256,8,256]{2,1,0:T(8,128)(2,1)} %x_in.1, bf16[8,9,32,32]{3,2,1,0:T(8,128)(2,1)} %conv_w.1, ...), custom_call_target="tpu_custom_call" | custom-call | tf_op jit(solution)/shard_map/pallas_call | solution.py:571
  32.6 1.4 %shard_map.105 = (bf16[256,8,256]{2,1,0:T(8,128)(2,1)}, f32[8,9,32,32]{3,2,1,0:T(8,128)}) custom-call(bf16[256,8,256]{2,1,0:T(8,128)(2,1)S(1)} %get-tuple-element.4.field, bf16[80,8,128]{2,1,0:T(8,128)(2,1)S(1)} %get-tuple-element.5.grad), custom_call_target="tpu_custom_call" | custom-call | tf_op jit(solution)/shard_map/pallas_call | solution.py:643
